TPU v7x, 128 devices: a whole 4x4x4 slice. The times are simulated.
128 devices in a mesh: dp: 8 (over y, core), ctx: 16 (over z, x).
Axes of the slice: x: 4, y: 4, z: 4, core: 2. Of those that a mesh axis runs over, the one named last changes fastest.
Arguments:
- queries: bfloat16 [8, 12288, 2048], P('dp', 'ctx'), may hold values from -6 to 6
- keys: bfloat16 [8, 12288, 2048], P('dp', 'ctx'), may hold values from -6 to 6
- values: bfloat16 [8, 12288, 2048], P('dp', 'ctx'), may hold values from -6 to 6
- grad_out: bfloat16 [8, 12288, 2048], P('dp', 'ctx'), may hold values from -6 to 6
- node_ids: int32 [8, 12288], P('dp', 'ctx'), may hold values from 0 to 767, never falling along the last dimension, each value on 1 to 64 neighbouring positions
- flags: int32 [8, 12288], P('dp', 'ctx'), may hold values 0 or 1
- gain: float32 [16], replicated, may hold values from 0.1 to 1.9
Outputs:
- grad_queries: bfloat16 [8, 12288, 2048], P('dp', 'ctx')
- grad_keys: bfloat16 [8, 12288, 2048], P('dp', 'ctx')
- grad_values: bfloat16 [8, 12288, 2048], P('dp', 'ctx')
- grad_gain: float32 [16], replicated
Inputs may be any that keep to these rules, and one draw needn't show every extreme that they name: `node_ids`: node numbers never fall along the tokens of a repository; a node spans 1 to 64 tokens.
All inputs are finite; a program needn't handle non-finite values. No bound on the sum of `flags` on one device may be relied on, other than what follows from the above.
Results may differ from a plain program's by a relative error of at most 0.0049.
Values sent between devices are 32-bit elements; how exact they have to be, the bound alone decides.
No kernel may reach another device: no remote copies, remote signals or barrier semaphores. Data moves between devices by JAX's collectives and lax.ppermute only.
A program may use at most 128 MiB of HBM per device.

v0:
```python
import math

import jax
import jax.numpy as jnp
from jax import lax
from jax.sharding import PartitionSpec as P

H = 16
HD = 128
BLOCK = 128


def shifted(block, axis, distance):
    devices = range(lax.axis_size(axis))
    route = [(i - distance, i) for i in devices if i - distance in devices]
    return lax.ppermute(block, axis, route)


def relay_forward(own):

    def advance(step, carry):
        message, total = carry
        message = shifted(message, "ctx", 1)
        return (message, total + message)

    steps = lax.axis_size("ctx") - 1
    return lax.fori_loop(0, steps, advance, (own, jnp.zeros_like(own)))[1]


def relay_backward(own):

    def advance(step, carry):
        message, total = carry
        message = shifted(message, "ctx", -1)
        return (message, total + message)

    steps = lax.axis_size("ctx") - 1
    return lax.fori_loop(0, steps, advance, (own, jnp.zeros_like(own)))[1]


def on_device(queries, keys, values, grad_out, node_ids, flags, gain):
    length = queries.shape[1]
    count = length // BLOCK
    scale = 1.0 / math.sqrt(HD * length * lax.axis_size("ctx"))
    q_blk = queries.reshape(count, BLOCK, H, HD)
    k_blk = keys.reshape(count, BLOCK, H, HD)
    v_blk = values.reshape(count, BLOCK, H, HD)
    g_blk = grad_out.reshape(count, BLOCK, H, HD)
    nodes = node_ids.reshape(count, BLOCK)
    marks = flags.reshape(count, BLOCK)
    rows = lax.broadcasted_iota(jnp.int32, (BLOCK, BLOCK), 0)
    cols = lax.broadcasted_iota(jnp.int32, (BLOCK, BLOCK), 1)
    causal = (cols <= rows)[None]
    linked = (nodes[:, :, None] == nodes[:, None, :]) | (marks[:, None, :] == 1)
    seen = (causal & linked).astype(jnp.float32)[:, None]
    kv_blk = jnp.einsum("bshd,bshe->bhde", k_blk, v_blk, preferred_element_type=jnp.float32)
    qg_blk = jnp.einsum("bthd,bthe->bhde", q_blk, g_blk, preferred_element_type=jnp.float32)
    own_kv = jnp.sum(kv_blk, axis=0)
    own_qg = jnp.sum(qg_blk, axis=0)
    carried = own_kv[None]
    before = relay_forward(carried)
    prior_kv = before[0]
    scores = jnp.einsum("bthd,bshd->bhts", q_blk, k_blk, preferred_element_type=jnp.float32) * seen
    dscores = jnp.einsum("bthd,bshd->bhts", g_blk, v_blk, preferred_element_type=jnp.float32) * seen
    intra_term = jnp.sum(scores * dscores, axis=(0, 2, 3))
    pm = scores.astype(jnp.bfloat16)
    dpm = dscores.astype(jnp.bfloat16)
    dq_near = jnp.einsum("bhts,bshd->bthd", dpm, k_blk, preferred_element_type=jnp.float32)
    dk_near = jnp.einsum("bhts,bthd->bshd", dpm, q_blk, preferred_element_type=jnp.float32)
    dv_near = jnp.einsum("bhts,bthd->bshd", pm, g_blk, preferred_element_type=jnp.float32)
    later_qg = relay_backward(own_qg[None])[0]
    zero = jnp.zeros((1,) + kv_blk.shape[1:], jnp.float32)
    prior = prior_kv[None] + jnp.cumsum(jnp.concatenate([zero, kv_blk[:-1]], axis=0), axis=0)
    later = later_qg[None] + jnp.flip(
        jnp.cumsum(jnp.flip(jnp.concatenate([qg_blk[1:], zero], axis=0), 0), axis=0), 0
    )
    inter_term = jnp.sum(prior * qg_blk, axis=(0, 2, 3))
    prior_h = prior.astype(jnp.bfloat16)
    later_h = later.astype(jnp.bfloat16)
    factor = (scale * gain)[None, None, :, None]
    dq = dq_near + jnp.einsum("bthe,bhde->bthd", g_blk, prior_h, preferred_element_type=jnp.float32)
    dk = dk_near + jnp.einsum("bshe,bhde->bshd", v_blk, later_h, preferred_element_type=jnp.float32)
    dv = dv_near + jnp.einsum("bshd,bhde->bshe", k_blk, later_h, preferred_element_type=jnp.float32)
    shape = queries.shape
    grad_queries = (dq * factor).astype(jnp.bfloat16).reshape(shape)
    grad_keys = (dk * factor).astype(jnp.bfloat16).reshape(shape)
    grad_values = (dv * factor).astype(jnp.bfloat16).reshape(shape)
    term = scale * (intra_term + inter_term)
    total = lax.psum(term, ("dp", "ctx"))
    norm_tokens = lax.axis_size("dp") * length * lax.axis_size("ctx") * HD
    grad_gain = total / math.sqrt(norm_tokens)
    return (grad_queries, grad_keys, grad_values, grad_gain)


def solution(mesh):
    placed = (
        P("dp", "ctx", None),
        P("dp", "ctx", None),
        P("dp", "ctx", None),
        P("dp", "ctx", None),
        P("dp", "ctx"),
        P("dp", "ctx"),
        P(),
    )
    return jax.shard_map(
        on_device,
        mesh=mesh,
        in_specs=placed,
        out_specs=(P("dp", "ctx", None), P("dp", "ctx", None), P("dp", "ctx", None), P()),
        check_vma=False,
    )
```

profile of v0, /device:TPU:1, one launch (start us, length us, event | category | flops | bytes accessed | tf_op | source)
XLA Modules:
  0.0 941.7 jit_solution(3516708746301565644)
XLA Ops:
  10.5 347.0 %while.26 = (s32[]{:T(128)}, f32[1,16,128,128]{3,2,1,0:T(8,128)S(1)}, f32[1,16,128,128]{3,2,1,0:T(8,128)S(1)}, s32[]{:T(128)}, s32[]{:T(128)}) while((s32[]{:T(128)}, f32[1,16,128,128]{3,2,1,0:T(8,128)S(1)}, f32[1,16,128,128]{3,2,1,0:T(8,128)S(1)}, s32[]{:T(128)}, s32[]{:T(128)}) %tuple.54), condition=%wide.region_2.0_spmd.clone, body=%wide.region_1.0_spmd.clone.sunk | while | flops 524291 | bytes 9437303 | solution.py:27
  14.5 21.7 %collective-permute-done = f32[1,16,128,128]{3,2,1,0:T(8,128)S(1)} collective-permute-done((f32[1,16,128,128]{3,2,1,0:T(8,128)S(1)}, f32[1,16,128,128]{3,2,1,0:T(8,128)S(1)}, u32[]{:S(2)}, u32[]{:S(2)}) %collective-permute-start) | collective-permute-done | bytes 1048608 | tf_op jit(solution)/shard_map/while/body/eval_jaxpr/ppermute | solution.py:16
  40.9 20.9 %collective-permute-done = f32[1,16,128,128]{3,2,1,0:T(8,128)S(1)} collective-permute-done((f32[1,16,128,128]{3,2,1,0:T(8,128)S(1)}, f32[1,16,128,128]{3,2,1,0:T(8,128)S(1)}, u32[]{:S(2)}, u32[]{:S(2)}) %collective-permute-start) | collective-permute-done | bytes 1048608 | tf_op jit(solution)/shard_map/while/body/eval_jaxpr/ppermute | solution.py:16
  66.4 20.0 %collective-permute-done = f32[1,16,128,128]{3,2,1,0:T(8,128)S(1)} collective-permute-done((f32[1,16,128,128]{3,2,1,0:T(8,128)S(1)}, f32[1,16,128,128]{3,2,1,0:T(8,128)S(1)}, u32[]{:S(2)}, u32[]{:S(2)}) %collective-permute-start) | collective-permute-done | bytes 1048608 | tf_op jit(solution)/shard_map/while/body/eval_jaxpr/ppermute | solution.py:16
  91.1 19.2 %collective-permute-done = f32[1,16,128,128]{3,2,1,0:T(8,128)S(1)} collective-permute-done((f32[1,16,128,128]{3,2,1,0:T(8,128)S(1)}, f32[1,16,128,128]{3,2,1,0:T(8,128)S(1)}, u32[]{:S(2)}, u32[]{:S(2)}) %collective-permute-start) | collective-permute-done | bytes 1048608 | tf_op jit(solution)/shard_map/while/body/eval_jaxpr/ppermute | solution.py:16
  115.0 18.3 %collective-permute-done = f32[1,16,128,128]{3,2,1,0:T(8,128)S(1)} collective-permute-done((f32[1,16,128,128]{3,2,1,0:T(8,128)S(1)}, f32[1,16,128,128]{3,2,1,0:T(8,128)S(1)}, u32[]{:S(2)}, u32[]{:S(2)}) %collective-permute-start) | collective-permute-done | bytes 1048608 | tf_op jit(solution)/shard_map/while/body/eval_jaxpr/ppermute | solution.py:16
  139.2 17.5 %collective-permute-done = f32[1,16,128,128]{3,2,1,0:T(8,128)S(1)} collective-permute-done((f32[1,16,128,128]{3,2,1,0:T(8,128)S(1)}, f32[1,16,128,128]{3,2,1,0:T(8,128)S(1)}, u32[]{:S(2)}, u32[]{:S(2)}) %collective-permute-start) | collective-permute-done | bytes 1048608 | tf_op jit(solution)/shard_map/while/body/eval_jaxpr/ppermute | solution.py:16
  425.2 382.0 %while.27 = (s32[]{:T(128)}, f32[1,16,128,128]{3,2,1,0:T(8,128)S(1)}, f32[1,16,128,128]{3,2,1,0:T(8,128)S(1)}, s32[]{:T(128)}, s32[]{:T(128)}) while((s32[]{:T(128)}, f32[1,16,128,128]{3,2,1,0:T(8,128)S(1)}, f32[1,16,128,128]{3,2,1,0:T(8,128)S(1)}, s32[]{:T(128)}, s32[]{:T(128)}) %tuple.53), condition=%wide.region_6.0_spmd.clone, body=%wide.region_5.0_spmd.clone.sunk | while | flops 524291 | bytes 9437303 | solution.py:38
  426.5 17.1 %collective-permute-done.1 = f32[1,16,128,128]{3,2,1,0:T(8,128)S(1)} collective-permute-done((f32[1,16,128,128]{3,2,1,0:T(8,128)S(1)}, f32[1,16,128,128]{3,2,1,0:T(8,128)S(1)}, u32[]{:S(2)}, u32[]{:S(2)}) %collective-permute-start.1) | collective-permute-done | bytes 1048608 | tf_op jit(solution)/shard_map/while/body/eval_jaxpr/ppermute | solution.py:16
  445.3 23.7 %collective-permute-done.1 = f32[1,16,128,128]{3,2,1,0:T(8,128)S(1)} collective-permute-done((f32[1,16,128,128]{3,2,1,0:T(8,128)S(1)}, f32[1,16,128,128]{3,2,1,0:T(8,128)S(1)}, u32[]{:S(2)}, u32[]{:S(2)}) %collective-permute-start.1) | collective-permute-done | bytes 1048608 | tf_op jit(solution)/shard_map/while/body/eval_jaxpr/ppermute | solution.py:16
  470.9 24.9 %collective-permute-done.1 = f32[1,16,128,128]{3,2,1,0:T(8,128)S(1)} collective-permute-done((f32[1,16,128,128]{3,2,1,0:T(8,128)S(1)}, f32[1,16,128,128]{3,2,1,0:T(8,128)S(1)}, u32[]{:S(2)}, u32[]{:S(2)}) %collective-permute-start.1) | collective-permute-done | bytes 1048608 | tf_op jit(solution)/shard_map/while/body/eval_jaxpr/ppermute | solution.py:16
  497.5 26.1 %collective-permute-done.1 = f32[1,16,128,128]{3,2,1,0:T(8,128)S(1)} collective-permute-done((f32[1,16,128,128]{3,2,1,0:T(8,128)S(1)}, f32[1,16,128,128]{3,2,1,0:T(8,128)S(1)}, u32[]{:S(2)}, u32[]{:S(2)}) %collective-permute-start.1) | collective-permute-done | bytes 1048608 | tf_op jit(solution)/shard_map/while/body/eval_jaxpr/ppermute | solution.py:16
  525.4 28.9 %collective-permute-done.1 = f32[1,16,128,128]{3,2,1,0:T(8,128)S(1)} collective-permute-done((f32[1,16,128,128]{3,2,1,0:T(8,128)S(1)}, f32[1,16,128,128]{3,2,1,0:T(8,128)S(1)}, u32[]{:S(2)}, u32[]{:S(2)}) %collective-permute-start.1) | collective-permute-done | bytes 1048608 | tf_op jit(solution)/shard_map/while/body/eval_jaxpr/ppermute | solution.py:16
  556.0 29.1 %collective-permute-done.1 = f32[1,16,128,128]{3,2,1,0:T(8,128)S(1)} collective-permute-done((f32[1,16,128,128]{3,2,1,0:T(8,128)S(1)}, f32[1,16,128,128]{3,2,1,0:T(8,128)S(1)}, u32[]{:S(2)}, u32[]{:S(2)}) %collective-permute-start.1) | collective-permute-done | bytes 1048608 | tf_op jit(solution)/shard_map/while/body/eval_jaxpr/ppermute | solution.py:16
  586.9 27.4 %collective-permute-done.1 = f32[1,16,128,128]{3,2,1,0:T(8,128)S(1)} collective-permute-done((f32[1,16,128,128]{3,2,1,0:T(8,128)S(1)}, f32[1,16,128,128]{3,2,1,0:T(8,128)S(1)}, u32[]{:S(2)}, u32[]{:S(2)}) %collective-permute-start.1) | collective-permute-done | bytes 1048608 | tf_op jit(solution)/shard_map/while/body/eval_jaxpr/ppermute | solution.py:16
  616.0 25.6 %collective-permute-done.1 = f32[1,16,128,128]{3,2,1,0:T(8,128)S(1)} collective-permute-done((f32[1,16,128,128]{3,2,1,0:T(8,128)S(1)}, f32[1,16,128,128]{3,2,1,0:T(8,128)S(1)}, u32[]{:S(2)}, u32[]{:S(2)}) %collective-permute-start.1) | collective-permute-done | bytes 1048608 | tf_op jit(solution)/shard_map/while/body/eval_jaxpr/ppermute | solution.py:16
  643.4 24.3 %collective-permute-done.1 = f32[1,16,128,128]{3,2,1,0:T(8,128)S(1)} collective-permute-done((f32[1,16,128,128]{3,2,1,0:T(8,128)S(1)}, f32[1,16,128,128]{3,2,1,0:T(8,128)S(1)}, u32[]{:S(2)}, u32[]{:S(2)}) %collective-permute-start.1) | collective-permute-done | bytes 1048608 | tf_op jit(solution)/shard_map/while/body/eval_jaxpr/ppermute | solution.py:16
  669.5 23.4 %collective-permute-done.1 = f32[1,16,128,128]{3,2,1,0:T(8,128)S(1)} collective-permute-done((f32[1,16,128,128]{3,2,1,0:T(8,128)S(1)}, f32[1,16,128,128]{3,2,1,0:T(8,128)S(1)}, u32[]{:S(2)}, u32[]{:S(2)}) %collective-permute-start.1) | collective-permute-done | bytes 1048608 | tf_op jit(solution)/shard_map/while/body/eval_jaxpr/ppermute | solution.py:16
  694.7 22.6 %collective-permute-done.1 = f32[1,16,128,128]{3,2,1,0:T(8,128)S(1)} collective-permute-done((f32[1,16,128,128]{3,2,1,0:T(8,128)S(1)}, f32[1,16,128,128]{3,2,1,0:T(8,128)S(1)}, u32[]{:S(2)}, u32[]{:S(2)}) %collective-permute-start.1) | collective-permute-done | bytes 1048608 | tf_op jit(solution)/shard_map/while/body/eval_jaxpr/ppermute | solution.py:16
  719.0 21.7 %collective-permute-done.1 = f32[1,16,128,128]{3,2,1,0:T(8,128)S(1)} collective-permute-done((f32[1,16,128,128]{3,2,1,0:T(8,128)S(1)}, f32[1,16,128,128]{3,2,1,0:T(8,128)S(1)}, u32[]{:S(2)}, u32[]{:S(2)}) %collective-permute-start.1) | collective-permute-done | bytes 1048608 | tf_op jit(solution)/shard_map/while/body/eval_jaxpr/ppermute | solution.py:16
  742.5 20.9 %collective-permute-done.1 = f32[1,16,128,128]{3,2,1,0:T(8,128)S(1)} collective-permute-done((f32[1,16,128,128]{3,2,1,0:T(8,128)S(1)}, f32[1,16,128,128]{3,2,1,0:T(8,128)S(1)}, u32[]{:S(2)}, u32[]{:S(2)}) %collective-permute-start.1) | collective-permute-done | bytes 1048608 | tf_op jit(solution)/shard_map/while/body/eval_jaxpr/ppermute | solution.py:16
  765.1 20.0 %collective-permute-done.1 = f32[1,16,128,128]{3,2,1,0:T(8,128)S(1)} collective-permute-done((f32[1,16,128,128]{3,2,1,0:T(8,128)S(1)}, f32[1,16,128,128]{3,2,1,0:T(8,128)S(1)}, u32[]{:S(2)}, u32[]{:S(2)}) %collective-permute-start.1) | collective-permute-done | bytes 1048608 | tf_op jit(solution)/shard_map/while/body/eval_jaxpr/ppermute | solution.py:16
  786.9 19.8 %collective-permute-done.1 = f32[1,16,128,128]{3,2,1,0:T(8,128)S(1)} collective-permute-done((f32[1,16,128,128]{3,2,1,0:T(8,128)S(1)}, f32[1,16,128,128]{3,2,1,0:T(8,128)S(1)}, u32[]{:S(2)}, u32[]{:S(2)}) %collective-permute-start.1) | collective-permute-done | bytes 1048608 | tf_op jit(solution)/shard_map/while/body/eval_jaxpr/ppermute | solution.py:16
  842.5 98.7 %psum.7 = f32[16]{0:T(128)S(1)} all-reduce(f32[16]{0:T(128)S(1)} %add_multiply_fusion), channel_id=1, replica_groups=mesh['dp'=8,'ctx'=16] {'dp','ctx'}, use_global_device_ids=true, to_apply=%region_10.11 | all-reduce | flops 16 | bytes 128 | tf_op jit(solution)/shard_map/psum | solution.py:89
  (175 shorter events, 367.7 us)
Async XLA Ops:
  10.5 25.7 %collective-permute-start = (f32[1,16,128,128]{3,2,1,0:T(8,128)S(1)}, f32[1,16,128,128]{3,2,1,0:T(8,128)S(1)}, u32[]{:S(2)}, u32[]{:S(2)}) collective-permute-start(f32[1,16,128,128]{3,2,1,0:T(8,128)S(1)} %get-tuple-element.127), channel_id=1, source_target_pairs={{0,1},{1,2},{2,3},{3,4},{4,5},{5,6},{6,7},{7,8},{8,9},{9,10},{10,1... | collective-permute-start | bytes 3145736 | tf_op jit(solution)/shard_map/while/body/eval_jaxpr/ppermute | solution.py:16
  36.7 25.1 %collective-permute-start = (f32[1,16,128,128]{3,2,1,0:T(8,128)S(1)}, f32[1,16,128,128]{3,2,1,0:T(8,128)S(1)}, u32[]{:S(2)}, u32[]{:S(2)}) collective-permute-start(f32[1,16,128,128]{3,2,1,0:T(8,128)S(1)} %get-tuple-element.127), channel_id=1, source_target_pairs={{0,1},{1,2},{2,3},{3,4},{4,5},{5,6},{6,7},{7,8},{8,9},{9,10},{10,1... | collective-permute-start | bytes 3145736 | tf_op jit(solution)/shard_map/while/body/eval_jaxpr/ppermute | solution.py:16
  62.2 24.2 %collective-permute-start = (f32[1,16,128,128]{3,2,1,0:T(8,128)S(1)}, f32[1,16,128,128]{3,2,1,0:T(8,128)S(1)}, u32[]{:S(2)}, u32[]{:S(2)}) collective-permute-start(f32[1,16,128,128]{3,2,1,0:T(8,128)S(1)} %get-tuple-element.127), channel_id=1, source_target_pairs={{0,1},{1,2},{2,3},{3,4},{4,5},{5,6},{6,7},{7,8},{8,9},{9,10},{10,1... | collective-permute-start | bytes 3145736 | tf_op jit(solution)/shard_map/while/body/eval_jaxpr/ppermute | solution.py:16
  86.9 23.4 %collective-permute-start = (f32[1,16,128,128]{3,2,1,0:T(8,128)S(1)}, f32[1,16,128,128]{3,2,1,0:T(8,128)S(1)}, u32[]{:S(2)}, u32[]{:S(2)}) collective-permute-start(f32[1,16,128,128]{3,2,1,0:T(8,128)S(1)} %get-tuple-element.127), channel_id=1, source_target_pairs={{0,1},{1,2},{2,3},{3,4},{4,5},{5,6},{6,7},{7,8},{8,9},{9,10},{10,1... | collective-permute-start | bytes 3145736 | tf_op jit(solution)/shard_map/while/body/eval_jaxpr/ppermute | solution.py:16
  110.8 22.5 %collective-permute-start = (f32[1,16,128,128]{3,2,1,0:T(8,128)S(1)}, f32[1,16,128,128]{3,2,1,0:T(8,128)S(1)}, u32[]{:S(2)}, u32[]{:S(2)}) collective-permute-start(f32[1,16,128,128]{3,2,1,0:T(8,128)S(1)} %get-tuple-element.127), channel_id=1, source_target_pairs={{0,1},{1,2},{2,3},{3,4},{4,5},{5,6},{6,7},{7,8},{8,9},{9,10},{10,1... | collective-permute-start | bytes 3145736 | tf_op jit(solution)/shard_map/while/body/eval_jaxpr/ppermute | solution.py:16
  133.7 23.0 %collective-permute-start = (f32[1,16,128,128]{3,2,1,0:T(8,128)S(1)}, f32[1,16,128,128]{3,2,1,0:T(8,128)S(1)}, u32[]{:S(2)}, u32[]{:S(2)}) collective-permute-start(f32[1,16,128,128]{3,2,1,0:T(8,128)S(1)} %get-tuple-element.127), channel_id=1, source_target_pairs={{0,1},{1,2},{2,3},{3,4},{4,5},{5,6},{6,7},{7,8},{8,9},{9,10},{10,1... | collective-permute-start | bytes 3145736 | tf_op jit(solution)/shard_map/while/body/eval_jaxpr/ppermute | solution.py:16
  157.2 22.9 %collective-permute-start = (f32[1,16,128,128]{3,2,1,0:T(8,128)S(1)}, f32[1,16,128,128]{3,2,1,0:T(8,128)S(1)}, u32[]{:S(2)}, u32[]{:S(2)}) collective-permute-start(f32[1,16,128,128]{3,2,1,0:T(8,128)S(1)} %get-tuple-element.127), channel_id=1, source_target_pairs={{0,1},{1,2},{2,3},{3,4},{4,5},{5,6},{6,7},{7,8},{8,9},{9,10},{10,1... | collective-permute-start | bytes 3145736 | tf_op jit(solution)/shard_map/while/body/eval_jaxpr/ppermute | solution.py:16
  180.5 22.1 %collective-permute-start = (f32[1,16,128,128]{3,2,1,0:T(8,128)S(1)}, f32[1,16,128,128]{3,2,1,0:T(8,128)S(1)}, u32[]{:S(2)}, u32[]{:S(2)}) collective-permute-start(f32[1,16,128,128]{3,2,1,0:T(8,128)S(1)} %get-tuple-element.127), channel_id=1, source_target_pairs={{0,1},{1,2},{2,3},{3,4},{4,5},{5,6},{6,7},{7,8},{8,9},{9,10},{10,1... | collective-permute-start | bytes 3145736 | tf_op jit(solution)/shard_map/while/body/eval_jaxpr/ppermute | solution.py:16
  289.6 21.3 %collective-permute-start = (f32[1,16,128,128]{3,2,1,0:T(8,128)S(1)}, f32[1,16,128,128]{3,2,1,0:T(8,128)S(1)}, u32[]{:S(2)}, u32[]{:S(2)}) collective-permute-start(f32[1,16,128,128]{3,2,1,0:T(8,128)S(1)} %get-tuple-element.127), channel_id=1, source_target_pairs={{0,1},{1,2},{2,3},{3,4},{4,5},{5,6},{6,7},{7,8},{8,9},{9,10},{10,1... | collective-permute-start | bytes 3145736 | tf_op jit(solution)/shard_map/while/body/eval_jaxpr/ppermute | solution.py:16
  311.3 22.2 %collective-permute-start = (f32[1,16,128,128]{3,2,1,0:T(8,128)S(1)}, f32[1,16,128,128]{3,2,1,0:T(8,128)S(1)}, u32[]{:S(2)}, u32[]{:S(2)}) collective-permute-start(f32[1,16,128,128]{3,2,1,0:T(8,128)S(1)} %get-tuple-element.127), channel_id=1, source_target_pairs={{0,1},{1,2},{2,3},{3,4},{4,5},{5,6},{6,7},{7,8},{8,9},{9,10},{10,1... | collective-permute-start | bytes 3145736 | tf_op jit(solution)/shard_map/while/body/eval_jaxpr/ppermute | solution.py:16
  334.0 23.0 %collective-permute-start = (f32[1,16,128,128]{3,2,1,0:T(8,128)S(1)}, f32[1,16,128,128]{3,2,1,0:T(8,128)S(1)}, u32[]{:S(2)}, u32[]{:S(2)}) collective-permute-start(f32[1,16,128,128]{3,2,1,0:T(8,128)S(1)} %get-tuple-element.127), channel_id=1, source_target_pairs={{0,1},{1,2},{2,3},{3,4},{4,5},{5,6},{6,7},{7,8},{8,9},{9,10},{10,1... | collective-permute-start | bytes 3145736 | tf_op jit(solution)/shard_map/while/body/eval_jaxpr/ppermute | solution.py:16
  444.0 25.0 %collective-permute-start.1 = (f32[1,16,128,128]{3,2,1,0:T(8,128)S(1)}, f32[1,16,128,128]{3,2,1,0:T(8,128)S(1)}, u32[]{:S(2)}, u32[]{:S(2)}) collective-permute-start(f32[1,16,128,128]{3,2,1,0:T(8,128)S(1)} %get-tuple-element.142), channel_id=1, source_target_pairs={{1,0},{2,1},{3,2},{4,3},{5,4},{6,5},{7,6},{8,7},{9,8},{10,9},{11,1... | collective-permute-start | bytes 3145736 | tf_op jit(solution)/shard_map/while/body/eval_jaxpr/ppermute | solution.py:16
  469.5 26.2 %collective-permute-start.1 = (f32[1,16,128,128]{3,2,1,0:T(8,128)S(1)}, f32[1,16,128,128]{3,2,1,0:T(8,128)S(1)}, u32[]{:S(2)}, u32[]{:S(2)}) collective-permute-start(f32[1,16,128,128]{3,2,1,0:T(8,128)S(1)} %get-tuple-element.142), channel_id=1, source_target_pairs={{1,0},{2,1},{3,2},{4,3},{5,4},{6,5},{7,6},{8,7},{9,8},{10,9},{11,1... | collective-permute-start | bytes 3145736 | tf_op jit(solution)/shard_map/while/body/eval_jaxpr/ppermute | solution.py:16
  496.2 27.4 %collective-permute-start.1 = (f32[1,16,128,128]{3,2,1,0:T(8,128)S(1)}, f32[1,16,128,128]{3,2,1,0:T(8,128)S(1)}, u32[]{:S(2)}, u32[]{:S(2)}) collective-permute-start(f32[1,16,128,128]{3,2,1,0:T(8,128)S(1)} %get-tuple-element.142), channel_id=1, source_target_pairs={{1,0},{2,1},{3,2},{4,3},{5,4},{6,5},{7,6},{8,7},{9,8},{10,9},{11,1... | collective-permute-start | bytes 3145736 | tf_op jit(solution)/shard_map/while/body/eval_jaxpr/ppermute | solution.py:16
  524.1 30.2 %collective-permute-start.1 = (f32[1,16,128,128]{3,2,1,0:T(8,128)S(1)}, f32[1,16,128,128]{3,2,1,0:T(8,128)S(1)}, u32[]{:S(2)}, u32[]{:S(2)}) collective-permute-start(f32[1,16,128,128]{3,2,1,0:T(8,128)S(1)} %get-tuple-element.142), channel_id=1, source_target_pairs={{1,0},{2,1},{3,2},{4,3},{5,4},{6,5},{7,6},{8,7},{9,8},{10,9},{11,1... | collective-permute-start | bytes 3145736 | tf_op jit(solution)/shard_map/while/body/eval_jaxpr/ppermute | solution.py:16
  554.7 30.4 %collective-permute-start.1 = (f32[1,16,128,128]{3,2,1,0:T(8,128)S(1)}, f32[1,16,128,128]{3,2,1,0:T(8,128)S(1)}, u32[]{:S(2)}, u32[]{:S(2)}) collective-permute-start(f32[1,16,128,128]{3,2,1,0:T(8,128)S(1)} %get-tuple-element.142), channel_id=1, source_target_pairs={{1,0},{2,1},{3,2},{4,3},{5,4},{6,5},{7,6},{8,7},{9,8},{10,9},{11,1... | collective-permute-start | bytes 3145736 | tf_op jit(solution)/shard_map/while/body/eval_jaxpr/ppermute | solution.py:16
  585.6 28.7 %collective-permute-start.1 = (f32[1,16,128,128]{3,2,1,0:T(8,128)S(1)}, f32[1,16,128,128]{3,2,1,0:T(8,128)S(1)}, u32[]{:S(2)}, u32[]{:S(2)}) collective-permute-start(f32[1,16,128,128]{3,2,1,0:T(8,128)S(1)} %get-tuple-element.142), channel_id=1, source_target_pairs={{1,0},{2,1},{3,2},{4,3},{5,4},{6,5},{7,6},{8,7},{9,8},{10,9},{11,1... | collective-permute-start | bytes 3145736 | tf_op jit(solution)/shard_map/while/body/eval_jaxpr/ppermute | solution.py:16
  614.7 26.9 %collective-permute-start.1 = (f32[1,16,128,128]{3,2,1,0:T(8,128)S(1)}, f32[1,16,128,128]{3,2,1,0:T(8,128)S(1)}, u32[]{:S(2)}, u32[]{:S(2)}) collective-permute-start(f32[1,16,128,128]{3,2,1,0:T(8,128)S(1)} %get-tuple-element.142), channel_id=1, source_target_pairs={{1,0},{2,1},{3,2},{4,3},{5,4},{6,5},{7,6},{8,7},{9,8},{10,9},{11,1... | collective-permute-start | bytes 3145736 | tf_op jit(solution)/shard_map/while/body/eval_jaxpr/ppermute | solution.py:16
  642.1 25.6 %collective-permute-start.1 = (f32[1,16,128,128]{3,2,1,0:T(8,128)S(1)}, f32[1,16,128,128]{3,2,1,0:T(8,128)S(1)}, u32[]{:S(2)}, u32[]{:S(2)}) collective-permute-start(f32[1,16,128,128]{3,2,1,0:T(8,128)S(1)} %get-tuple-element.142), channel_id=1, source_target_pairs={{1,0},{2,1},{3,2},{4,3},{5,4},{6,5},{7,6},{8,7},{9,8},{10,9},{11,1... | collective-permute-start | bytes 3145736 | tf_op jit(solution)/shard_map/while/body/eval_jaxpr/ppermute | solution.py:16
  668.2 24.7 %collective-permute-start.1 = (f32[1,16,128,128]{3,2,1,0:T(8,128)S(1)}, f32[1,16,128,128]{3,2,1,0:T(8,128)S(1)}, u32[]{:S(2)}, u32[]{:S(2)}) collective-permute-start(f32[1,16,128,128]{3,2,1,0:T(8,128)S(1)} %get-tuple-element.142), channel_id=1, source_target_pairs={{1,0},{2,1},{3,2},{4,3},{5,4},{6,5},{7,6},{8,7},{9,8},{10,9},{11,1... | collective-permute-start | bytes 3145736 | tf_op jit(solution)/shard_map/while/body/eval_jaxpr/ppermute | solution.py:16
  693.4 23.9 %collective-permute-start.1 = (f32[1,16,128,128]{3,2,1,0:T(8,128)S(1)}, f32[1,16,128,128]{3,2,1,0:T(8,128)S(1)}, u32[]{:S(2)}, u32[]{:S(2)}) collective-permute-start(f32[1,16,128,128]{3,2,1,0:T(8,128)S(1)} %get-tuple-element.142), channel_id=1, source_target_pairs={{1,0},{2,1},{3,2},{4,3},{5,4},{6,5},{7,6},{8,7},{9,8},{10,9},{11,1... | collective-permute-start | bytes 3145736 | tf_op jit(solution)/shard_map/while/body/eval_jaxpr/ppermute | solution.py:16
  717.7 23.0 %collective-permute-start.1 = (f32[1,16,128,128]{3,2,1,0:T(8,128)S(1)}, f32[1,16,128,128]{3,2,1,0:T(8,128)S(1)}, u32[]{:S(2)}, u32[]{:S(2)}) collective-permute-start(f32[1,16,128,128]{3,2,1,0:T(8,128)S(1)} %get-tuple-element.142), channel_id=1, source_target_pairs={{1,0},{2,1},{3,2},{4,3},{5,4},{6,5},{7,6},{8,7},{9,8},{10,9},{11,1... | collective-permute-start | bytes 3145736 | tf_op jit(solution)/shard_map/while/body/eval_jaxpr/ppermute | solution.py:16
  741.2 22.2 %collective-permute-start.1 = (f32[1,16,128,128]{3,2,1,0:T(8,128)S(1)}, f32[1,16,128,128]{3,2,1,0:T(8,128)S(1)}, u32[]{:S(2)}, u32[]{:S(2)}) collective-permute-start(f32[1,16,128,128]{3,2,1,0:T(8,128)S(1)} %get-tuple-element.142), channel_id=1, source_target_pairs={{1,0},{2,1},{3,2},{4,3},{5,4},{6,5},{7,6},{8,7},{9,8},{10,9},{11,1... | collective-permute-start | bytes 3145736 | tf_op jit(solution)/shard_map/while/body/eval_jaxpr/ppermute | solution.py:16
  763.8 21.3 %collective-permute-start.1 = (f32[1,16,128,128]{3,2,1,0:T(8,128)S(1)}, f32[1,16,128,128]{3,2,1,0:T(8,128)S(1)}, u32[]{:S(2)}, u32[]{:S(2)}) collective-permute-start(f32[1,16,128,128]{3,2,1,0:T(8,128)S(1)} %get-tuple-element.142), channel_id=1, source_target_pairs={{1,0},{2,1},{3,2},{4,3},{5,4},{6,5},{7,6},{8,7},{9,8},{10,9},{11,1... | collective-permute-start | bytes 3145736 | tf_op jit(solution)/shard_map/while/body/eval_jaxpr/ppermute | solution.py:16
  (26 other events, 267.0 us)
where the time goes:
time: 943 us; the launch traced here: 942 us
  waiting for transfers between devices  613 us (65%)
  starting transfers between devices  102 us (11%)
  blocking collectives  98.7 us (10%)
  matrix products  51.5 us (5%)
  local copies, waits for them, and re-layouts  49.9 us (5%)
  other arithmetic  24.8 us (3%)
    ppermute x30, waiting for transfers between devices, shifted(): return lax.ppermute(block, axis, route)  613 us
    ppermute x30, starting transfers between devices, shifted(): return lax.ppermute(block, axis, route)  102 us
    psum x1, blocking collectives, on_device(): total = lax.psum(term, ('dp', 'ctx'))  98.7 us
  transfers between devices with their start and end apart: 30, of which 30 were waited for; matrix products, arithmetic and copies ran while one was open for 0% of the time, Pallas kernels for 0%

commit v1 on v0

v1 whole, which is shorter than its diff:
```python
import functools
import math

import jax
import jax.numpy as jnp
from jax import lax
from jax.experimental import pallas as pl
from jax.experimental.pallas import tpu as pltpu
from jax.sharding import PartitionSpec as P

H = 16
HD = 128
BLOCK = 128
TILE = 8


def dot(a, b, dims):
    return lax.dot_general(a, b, (dims, ((), ())), preferred_element_type=jnp.float32)


def over_rows(a, b):
    return dot(a, b, ((0,), (0,)))


def over_cols(a, b):
    return dot(a, b, ((1,), (1,)))


def plain(a, b):
    return dot(a, b, ((1,), (0,)))


def head(ref, j, rows=slice(None)):
    return ref[rows, j * HD:(j + 1) * HD]


def parted(state):
    high = state.astype(jnp.bfloat16)
    return high, (state - high.astype(jnp.float32)).astype(jnp.bfloat16)


def times_transposed(rows, parts):
    return over_cols(jnp.concatenate([rows, rows], axis=1), jnp.concatenate(parts, axis=1))


def times(rows, parts):
    return plain(jnp.concatenate([rows, rows], axis=1), jnp.concatenate(parts, axis=0))


def cost(flops, bytes_accessed):
    return pl.CostEstimate(flops=flops, bytes_accessed=bytes_accessed, transcendentals=0)


FULL = 60 * 1024 * 1024


def params(vmem):
    return pltpu.CompilerParams(vmem_limit_bytes=vmem)


CHUNKS = 8


def state_kernel(*refs):
    sources, out_ref, kept, sems = refs[:4], refs[4], refs[5:9], refs[9]
    wide = sources[0].shape[2] // CHUNKS
    heads = wide // HD

    def copy(i, n):
        columns = slice(n * wide, (n + 1) * wide)
        return pltpu.make_async_copy(
            sources[i].at[0, :, columns], kept[i].at[:, columns], sems.at[i, n]
        )

    for n in range(CHUNKS):
        for i in range(4):
            copy(i, n).start()
    for n in range(CHUNKS):
        for i in range(4):
            copy(i, n).wait()
        for j in range(n * heads, (n + 1) * heads):
            q, k, v, g = (head(ref, j) for ref in kept)
            out_ref[j, 0:HD] = over_rows(k, v)
            out_ref[j, HD:2 * HD] = over_rows(q, g)


def own_states(q, k, v, g):
    _, length, features = q.shape
    return pl.pallas_call(
        state_kernel,
        in_specs=[pl.BlockSpec(memory_space=pltpu.HBM)] * 4,
        out_specs=pl.BlockSpec(memory_space=pltpu.VMEM),
        out_shape=jax.ShapeDtypeStruct((H, 2 * HD, HD), jnp.float32),
        scratch_shapes=[pltpu.VMEM((length, features), jnp.bfloat16)] * 4
        + [pltpu.SemaphoreType.DMA((4, CHUNKS))],
        compiler_params=params(FULL),
        cost_estimate=cost(4 * length * H * HD * HD, 8 * length * H * HD),
        name="own_states",
    )(q, k, v, g)


NEAR_HEADS = 1


def rows_of(b):
    return slice(b * BLOCK, (b + 1) * BLOCK)


def visible(nodes_ref, marks_ref, b):
    rows = lax.broadcasted_iota(jnp.int32, (BLOCK, BLOCK), 0)
    cols = lax.broadcasted_iota(jnp.int32, (BLOCK, BLOCK), 1)
    across = jnp.broadcast_to(nodes_ref[0:1, rows_of(b)], (BLOCK, BLOCK))
    marks = jnp.broadcast_to(marks_ref[0:1, rows_of(b)], (BLOCK, BLOCK))
    return ((cols <= rows) & ((across == across.T) | (marks == 1))).astype(jnp.float32)


def near_q_kernel(count, q_ref, k_ref, v_ref, g_ref, nodes_ref, marks_ref, dq_ref, term_ref, seen_ref):
    @pl.when(pl.program_id(0) == 0)
    def _():
        for b in range(count):
            seen_ref[b] = visible(nodes_ref, marks_ref, b)

    for j in range(NEAR_HEADS):
        term = jnp.zeros((BLOCK, BLOCK), jnp.float32)
        earlier = None
        for b in range(count):
            q, k, v, g = (head(ref, j, rows_of(b)) for ref in (q_ref, k_ref, v_ref, g_ref))
            seen = seen_ref[b]
            dscores = over_cols(g, v) * seen
            term = term + over_cols(q, k) * dscores
            dq = plain(dscores.astype(jnp.bfloat16), k)
            if earlier is not None:
                term = term + earlier * over_rows(q, g)
                dq = dq + times_transposed(g, parted(earlier))
            dq_ref[rows_of(b), j * HD:(j + 1) * HD] = dq
            if b < count - 1:
                kv = over_rows(k, v)
                earlier = kv if earlier is None else earlier + kv
        term_ref[j] = jnp.sum(term.reshape(BLOCK // 8, 8, BLOCK), axis=0)


def near_kv_kernel(count, q_ref, k_ref, v_ref, g_ref, nodes_ref, marks_ref, dk_ref, dv_ref, seen_ref):
    @pl.when(pl.program_id(0) == 0)
    def _():
        for b in range(count):
            seen_ref[b] = visible(nodes_ref, marks_ref, b).T

    for j in range(NEAR_HEADS):
        later = None
        for b in reversed(range(count)):
            q, k, v, g = (head(ref, j, rows_of(b)) for ref in (q_ref, k_ref, v_ref, g_ref))
            seen = seen_ref[b]
            dk = plain((over_cols(v, g) * seen).astype(jnp.bfloat16), q)
            dv = plain((over_cols(k, q) * seen).astype(jnp.bfloat16), g)
            if later is not None:
                parts = parted(later)
                dk = dk + times_transposed(v, parts)
                dv = dv + times(k, parts)
            dk_ref[rows_of(b), j * HD:(j + 1) * HD] = dk
            dv_ref[rows_of(b), j * HD:(j + 1) * HD] = dv
            if b > 0:
                qg = over_rows(q, g)
                later = qg if later is None else later + qg


def near(kernel, inputs, nodes, marks, outputs, terms, name):
    _, length, features = inputs[0].shape
    count = length // BLOCK
    wide = pl.BlockSpec((None, length, NEAR_HEADS * HD), lambda i: (0, 0, i))
    flat = pl.BlockSpec((1, length), lambda i: (0, 0))
    term = pl.BlockSpec((NEAR_HEADS, 8, BLOCK), lambda i: (i, 0, 0))
    return pl.pallas_call(
        functools.partial(kernel, count),
        grid=(H // NEAR_HEADS,),
        in_specs=[wide] * 4 + [flat] * 2,
        out_specs=[wide] * outputs + [term] * terms,
        out_shape=[jax.ShapeDtypeStruct((1, length, features), jnp.float32)] * outputs
        + [jax.ShapeDtypeStruct((H, 8, BLOCK), jnp.float32)] * terms,
        scratch_shapes=[pltpu.VMEM((count, BLOCK, BLOCK), jnp.float32)],
        compiler_params=params(FULL),
        cost_estimate=cost(28 * length * H * HD * HD, 20 * length * H * HD),
        name=name,
    )(*inputs, nodes, marks)


def scan_kernel(spot_ref, own_ref, local_ref, out_ref):
    devices = own_ref.shape[0]
    total = jnp.zeros((HD, HD), jnp.float32)
    cross = jnp.zeros((HD, HD), jnp.float32)
    for at in range(devices):
        out_ref[at, 0:HD] = total
        cross = cross + total * own_ref[at, HD:2 * HD]
        total = total + own_ref[at, 0:HD]
    total = jnp.zeros((HD, HD), jnp.float32)
    for at in reversed(range(devices)):
        out_ref[at, HD:2 * HD] = total
        total = total + own_ref[at, HD:2 * HD]
    cross = jnp.sum(jnp.sum(cross, axis=0, keepdims=True), axis=1, keepdims=True)
    lanes = lax.broadcasted_iota(jnp.int32, (TILE, HD), 1)
    terms = local_ref[...] + jnp.where(lanes == spot_ref[0], cross, 0.0)
    for at in range(devices):
        out_ref[at, 2 * HD:2 * HD + TILE] = terms


def scan(spot, own, local):
    whole = pl.BlockSpec(memory_space=pltpu.VMEM)
    return pl.pallas_call(
        scan_kernel,
        in_specs=[pl.BlockSpec(memory_space=pltpu.SMEM), whole, whole],
        out_specs=whole,
        out_shape=jax.ShapeDtypeStruct((own.shape[0], 2 * HD + TILE, HD), jnp.float32),
        compiler_params=params(FULL),
        cost_estimate=cost(3 * own.size, 8 * own.size),
        name="scan",
    )(spot, own, local)


FAR_HEADS = 2


def far_kernel(scale, gain_ref, k_ref, v_ref, g_ref, part_q_ref, part_k_ref, part_v_ref, state_ref,
               dq_ref, dk_ref, dv_ref):
    for j in range(FAR_HEADS):
        columns = slice(j * HD, (j + 1) * HD)
        factor = gain_ref[pl.program_id(0) * FAR_HEADS + j] * scale
        prior = parted(state_ref[j, 0:HD])
        later = parted(state_ref[j, HD:2 * HD])
        dq = part_q_ref[:, columns] + times_transposed(g_ref[:, columns], prior)
        dq_ref[:, columns] = (dq * factor).astype(jnp.bfloat16)
        dk = part_k_ref[:, columns] + times_transposed(v_ref[:, columns], later)
        dk_ref[:, columns] = (dk * factor).astype(jnp.bfloat16)
        dv = part_v_ref[:, columns] + times(k_ref[:, columns], later)
        dv_ref[:, columns] = (dv * factor).astype(jnp.bfloat16)


def far(scale, gain, k, v, g, parts, states):
    _, length, features = k.shape
    wide = pl.BlockSpec((None, length, FAR_HEADS * HD), lambda i: (0, 0, i))
    state = pl.BlockSpec((FAR_HEADS, 2 * HD, HD), lambda i: (i, 0, 0))
    return pl.pallas_call(
        functools.partial(far_kernel, scale),
        grid=(H // FAR_HEADS,),
        in_specs=[pl.BlockSpec(memory_space=pltpu.SMEM)] + [wide] * 6 + [state],
        out_specs=[wide] * 3,
        out_shape=[jax.ShapeDtypeStruct((1, length, features), jnp.bfloat16)] * 3,
        compiler_params=params(FULL),
        cost_estimate=cost(12 * length * H * HD * HD, 24 * length * H * HD),
        name="far",
    )(gain, k, v, g, *parts, states)


def exchange(block, axis):
    return lax.all_to_all(block, axis, 0, 0, tiled=True)


def on_device(queries, keys, values, grad_out, node_ids, flags, gain):
    length = queries.shape[1]
    scale = 1.0 / math.sqrt(HD * length * lax.axis_size("ctx"))
    spot = lax.axis_index("ctx").astype(jnp.int32)[None]

    inputs = (queries, keys, values, grad_out)
    owned = exchange(own_states(*inputs), "ctx")
    part_q, own_term = near(near_q_kernel, inputs, node_ids, flags, 1, 1, "near_q")
    part_k, part_v = near(near_kv_kernel, inputs, node_ids, flags, 2, 0, "near_kv")
    local = jnp.pad(jnp.sum(own_term, axis=(1, 2)), (0, HD - H))[None]
    states = exchange(scan(spot, owned, jnp.broadcast_to(local, (TILE, HD))), "ctx")

    terms = jnp.sum(states[:, 2 * HD:, :], axis=0)
    terms = exchange(jnp.broadcast_to(terms, (lax.axis_size("dp"), TILE, HD)), "dp")
    norm_tokens = lax.axis_size("dp") * length * lax.axis_size("ctx") * HD
    grad_gain = jnp.sum(terms, axis=0)[0, :H] * scale / math.sqrt(norm_tokens)

    return (*far(scale, gain, keys, values, grad_out, (part_q, part_k, part_v), states), grad_gain)


def solution(mesh):
    placed = (
        P("dp", "ctx", None),
        P("dp", "ctx", None),
        P("dp", "ctx", None),
        P("dp", "ctx", None),
        P("dp", "ctx"),
        P("dp", "ctx"),
        P(),
    )
    return jax.shard_map(
        on_device,
        mesh=mesh,
        in_specs=placed,
        out_specs=(P("dp", "ctx", None), P("dp", "ctx", None), P("dp", "ctx", None), P()),
        check_vma=False,
    )
```

time: 943 us -> 111 us (0.12)
  waiting for transfers between devices: 613 us -> 10.6 us
  blocking collectives: 98.7 us -> 0 us
  starting transfers between devices: 102 us -> 19.7 us
  Pallas kernels: 0 us -> 75.4 us
  matrix products: 51.5 us -> 0 us
  local copies, waits for them, and re-layouts: 49.9 us -> 2.01 us
  other arithmetic: 24.8 us -> 1.58 us
    ppermute x30 -> x0, waiting for transfers between devices: 613 us -> none  [shifted(): return lax.ppermute(block, axis, route)]
    ppermute x30 -> x0, starting transfers between devices: 102 us -> none  [shifted(): return lax.ppermute(block, axis, route)]
    psum x1 -> x0, blocking collectives: 98.7 us -> none  [on_device(): total = lax.psum(term, ('dp', 'ctx'))]
    pallas_call x0 -> x5, Pallas kernels: none -> 75.4 us  [the longest x2 48.9 us: near(): pl.pallas_call(functools.partial(kernel, count), grid=(H // NEAR_HEADS,),...]
    dot_general x10 -> x0, matrix products: 51.5 us -> none  [the longest x1 7.99 us: on_device(): jnp.einsum('bhts,bthd->bshd', dpm, q_blk, preferred_element_type=jnp.floa...]
    all_to_all x0 -> x3, starting transfers between devices: none -> 19.7 us  [exchange(): return lax.all_to_all(block, axis, 0, 0, tiled=True)]
    reshape x3 -> x0, local copies, waits for them, and re-layouts: 15 us -> none  [the longest x1 5.93 us: on_device(): grad_keys = (dk * factor).astype(jnp.bfloat16).reshape(shape)]
    unnamed x44 -> x4, local copies, waits for them, and re-layouts: 12.9 us -> 0.7 us
  transfers between devices with their start and end apart: 30 -> 3, of which waited for: 30 -> 2; matrix products, arithmetic and copies ran while one was open for 0% -> 1% of each run, Pallas kernels for 0% -> 59%
where the time goes in v1:
time: 111 us; the launch traced here: 110 us
  Pallas kernels  75.4 us (68%)
  starting transfers between devices  19.7 us (18%)
  waiting for transfers between devices  10.6 us (10%)
  local copies, waits for them, and re-layouts  2.01 us (2%)
  other arithmetic  1.58 us (1%)
    pallas_call x2, Pallas kernels, near(): pl.pallas_call(functools.partial(kernel, count), grid=(H // NEAR_HEADS,),...  48.9 us
    all_to_all x3, starting transfers between devices, exchange(): return lax.all_to_all(block, axis, 0, 0, tiled=True)  19.7 us
    pallas_call x1, Pallas kernels, far(): pl.pallas_call(functools.partial(far_kernel, scale), grid=(H // FAR_HEADS...  15.9 us
    all_to_all x3, waiting for transfers between devices, exchange(): return lax.all_to_all(block, axis, 0, 0, tiled=True)  10.6 us
    pallas_call x1, Pallas kernels, own_states(): pl.pallas_call(state_kernel, in_specs=[pl.BlockSpec(memory_space=pltpu.HB...  7.4 us
    pallas_call x1, Pallas kernels, scan(): pl.pallas_call(scan_kernel, in_specs=[pl.BlockSpec(memory_space=pltpu.SME...  3.21 us
  transfers between devices with their start and end apart: 3, of which 2 were waited for; matrix products, arithmetic and copies ran while one was open for 1% of the time, Pallas kernels for 59%

profile of v1, /device:TPU:1, one launch (start us, length us, event | category | flops | bytes accessed | tf_op | source)
XLA Modules:
  0.0 110.1 jit_solution(12772144927451300738)
XLA Ops:
  0.6 7.4 %own_states.1 = f32[16,256,128]{2,1,0:T(8,128)} custom-call(bf16[1,768,2048]{2,1,0:T(8,128)(2,1)} %refs_0_.1, bf16[1,768,2048]{2,1,0:T(8,128)(2,1)} %k_ref.5, bf16[1,768,2048]{2,1,0:T(8,128)(2,1)} %v_ref.5, bf16[1,768,2048]{2,1,0:T(8,128)(2,1)} %g_ref.5), custom_call_target="tpu_custom_call" | custom-call | flops 805306368 | bytes 12582912 | tf_op jit(solution)/shard_map/own_states/pallas_call | solution.py:89
  8.0 8.4 %all-to-all-start = ((f32[16,256,128]{2,1,0:T(8,128)}), f32[16,256,128]{2,1,0:T(8,128)S(1)}, u32[]{:S(2)}, u32[]{:S(2)}) async-start(f32[16,256,128]{2,1,0:T(8,128)} %own_states.1), calls=%async_computation | async-start | bytes 4194304 | tf_op jit(solution)/shard_map/all_to_all | solution.py:253
  16.5 22.1 %near_q.1 = (f32[1,768,2048]{2,1,0:T(8,128)}, f32[16,8,128]{2,1,0:T(8,128)}) custom-call(bf16[1,768,2048]{2,1,0:T(8,128)(2,1)} %refs_0_.1, bf16[1,768,2048]{2,1,0:T(8,128)(2,1)} %k_ref.5, bf16[1,768,2048]{2,1,0:T(8,128)(2,1)} %v_ref.5, bf16[1,768,2048]{2,1,0:T(8,128)(2,1)} %g_ref.5, s32[1,768]{1,0:T(1,128)} %nodes_ref.3, s32[1,768]{1,0:T(1,128)} %marks_ref.3), custom_call_target="tpu_custom_call" | custom-call | flops 5637144576 | bytes 31457280 | tf_op jit(solution)/shard_map/near_q/pallas_call | solution.py:172
  38.6 1.0 reduce_sum.27
  39.6 7.8 %all-to-all-done.own_ref = f32[16,256,128]{2,1,0:T(8,128)S(1)} async-done(((f32[16,256,128]{2,1,0:T(8,128)}), f32[16,256,128]{2,1,0:T(8,128)S(1)}, u32[]{:S(2)}, u32[]{:S(2)}) %all-to-all-start) | async-done | bytes 2097184 | tf_op jit(solution)/shard_map/all_to_all | solution.py:253
  47.4 0.0 copy-start.1
  47.4 0.6 broadcast_in_dim.13.local_ref
  48.1 0.7 copy-done.1
  48.8 3.2 %scan.1 = f32[16,264,128]{2,1,0:T(8,128)} custom-call(s32[1]{0:T(128)} %bitcast.spot_ref, f32[16,256,128]{2,1,0:T(8,128)} %copy-done.1, f32[8,128]{1,0:T(8,128)} %broadcast_in_dim.13.local_ref), custom_call_target="tpu_custom_call" | custom-call | flops 1572864 | bytes 4194304 | tf_op jit(solution)/shard_map/scan/pallas_call | solution.py:207
  52.0 3.8 %all-to-all-start.1 = ((f32[16,264,128]{2,1,0:T(8,128)}), f32[16,264,128]{2,1,0:T(8,128)S(1)}, u32[]{:S(2)}, u32[]{:S(2)}) async-start(f32[16,264,128]{2,1,0:T(8,128)} %scan.1), calls=%async_computation.1 | async-start | bytes 4325376 | tf_op jit(solution)/shard_map/all_to_all | solution.py:253
  55.8 26.8 %near_kv.1 = (f32[1,768,2048]{2,1,0:T(8,128)}, f32[1,768,2048]{2,1,0:T(8,128)}) custom-call(bf16[1,768,2048]{2,1,0:T(8,128)(2,1)} %refs_0_.1, bf16[1,768,2048]{2,1,0:T(8,128)(2,1)} %k_ref.5, bf16[1,768,2048]{2,1,0:T(8,128)(2,1)} %v_ref.5, bf16[1,768,2048]{2,1,0:T(8,128)(2,1)} %g_ref.5, s32[1,768]{1,0:T(1,128)} %nodes_ref.3, s32[1,768]{1,0:T(1,128)} %marks_ref.3), custom_call_target="tpu_custom_call" | custom-call | flops 5637144576 | bytes 31457280 | tf_op jit(solution)/shard_map/near_kv/pallas_call | solution.py:172
  82.6 2.8 %all-to-all-done.1.state_ref = f32[16,264,128]{2,1,0:T(8,128)S(1)} async-done(((f32[16,264,128]{2,1,0:T(8,128)}), f32[16,264,128]{2,1,0:T(8,128)S(1)}, u32[]{:S(2)}, u32[]{:S(2)}) %all-to-all-start.1) | async-done | bytes 2162720 | tf_op jit(solution)/shard_map/all_to_all | solution.py:253
  85.4 0.0 copy-start
  85.4 0.7 broadcast_in_dim.14
  86.1 7.5 %all-to-all-start.2 = ((f32[8,8,128]{2,1,0:T(8,128)}), f32[8,8,128]{2,1,0:T(8,128)S(1)}, u32[]{:S(2)}, u32[]{:S(2)}) async-start(f32[8,8,128]{2,1,0:T(8,128)} %broadcast_in_dim.14), calls=%async_computation.2 | async-start | bytes 65536 | tf_op jit(solution)/shard_map/all_to_all | solution.py:253
  93.6 0.0 copy-done
  93.6 15.9 %far.1 = (bf16[1,768,2048]{2,1,0:T(8,128)(2,1)}, bf16[1,768,2048]{2,1,0:T(8,128)(2,1)}, bf16[1,768,2048]{2,1,0:T(8,128)(2,1)}) custom-call(f32[16]{0:T(128)} %gain_ref.1, bf16[1,768,2048]{2,1,0:T(8,128)(2,1)} %k_ref.5, bf16[1,768,2048]{2,1,0:T(8,128)(2,1)} %v_ref.5, bf16[1,768,2048]{2,1,0:T(8,128)(2,1)} %g_ref.5, ...), custom_call_target="tpu_custom_call" | custom-call | flops 2415919104 | bytes 37748736 | tf_op jit(solution)/shard_map/far/pallas_call | solution.py:240
  109.5 0.0 all-to-all-done.2
  109.5 0.5 multiply_bitcast_fusion
  (3 shorter events, 0.0 us)
Async XLA Ops:
  8.0 39.4 %all-to-all-start = ((f32[16,256,128]{2,1,0:T(8,128)}), f32[16,256,128]{2,1,0:T(8,128)S(1)}, u32[]{:S(2)}, u32[]{:S(2)}) async-start(f32[16,256,128]{2,1,0:T(8,128)} %own_states.1), calls=%async_computation | async-start | bytes 4194304 | tf_op jit(solution)/shard_map/all_to_all | solution.py:253
  47.4 1.3 %copy-start.1 = (f32[16,256,128]{2,1,0:T(8,128)}, f32[16,256,128]{2,1,0:T(8,128)S(1)}, u32[]{:S(2)}) copy-start(f32[16,256,128]{2,1,0:T(8,128)S(1)} %all-to-all-done.own_ref) | copy-start | bytes 6291460
  52.0 33.4 %all-to-all-start.1 = ((f32[16,264,128]{2,1,0:T(8,128)}), f32[16,264,128]{2,1,0:T(8,128)S(1)}, u32[]{:S(2)}, u32[]{:S(2)}) async-start(f32[16,264,128]{2,1,0:T(8,128)} %scan.1), calls=%async_computation.1 | async-start | bytes 4325376 | tf_op jit(solution)/shard_map/all_to_all | solution.py:253
  85.4 8.2 %copy-start = (f32[16,264,128]{2,1,0:T(8,128)}, f32[16,264,128]{2,1,0:T(8,128)S(1)}, u32[]{:S(2)}) copy-start(f32[16,264,128]{2,1,0:T(8,128)S(1)} %all-to-all-done.1.state_ref) | copy-start | bytes 6488068
  86.1 23.4 %all-to-all-start.2 = ((f32[8,8,128]{2,1,0:T(8,128)}), f32[8,8,128]{2,1,0:T(8,128)S(1)}, u32[]{:S(2)}, u32[]{:S(2)}) async-start(f32[8,8,128]{2,1,0:T(8,128)} %broadcast_in_dim.14), calls=%async_computation.2 | async-start | bytes 65536 | tf_op jit(solution)/shard_map/all_to_all | solution.py:253

commit v2 on v1

--- a/solution.py
+++ b/solution.py
@@ -58,7 +58,7 @@
     return pltpu.CompilerParams(vmem_limit_bytes=vmem)
 
 
-CHUNKS = 8
+CHUNKS = 4
 
 
 def state_kernel(*refs):
@@ -99,7 +99,11 @@
     )(q, k, v, g)
 
 
-NEAR_HEADS = 1
+NEAR_HEADS = 2
+
+
+def summed(block):
+    return jnp.sum(jnp.sum(block, axis=0, keepdims=True), axis=1, keepdims=True)
 
 
 def rows_of(b):
@@ -119,6 +123,7 @@
     def _():
         for b in range(count):
             seen_ref[b] = visible(nodes_ref, marks_ref, b)
+        term_ref[...] = jnp.zeros_like(term_ref)
 
     for j in range(NEAR_HEADS):
         term = jnp.zeros((BLOCK, BLOCK), jnp.float32)
@@ -132,11 +137,13 @@
             if earlier is not None:
                 term = term + earlier * over_rows(q, g)
                 dq = dq + times_transposed(g, parted(earlier))
-            dq_ref[rows_of(b), j * HD:(j + 1) * HD] = dq
+            dq_ref[rows_of(b), j * HD:(j + 1) * HD] = dq.astype(jnp.bfloat16)
             if b < count - 1:
                 kv = over_rows(k, v)
                 earlier = kv if earlier is None else earlier + kv
-        term_ref[j] = jnp.sum(term.reshape(BLOCK // 8, 8, BLOCK), axis=0)
+        lanes = lax.broadcasted_iota(jnp.int32, (TILE, HD), 1)
+        here = lanes == pl.program_id(0) * NEAR_HEADS + j
+        term_ref[...] += jnp.where(here, summed(term), 0.0)
 
 
 def near_kv_kernel(count, q_ref, k_ref, v_ref, g_ref, nodes_ref, marks_ref, dk_ref, dv_ref, seen_ref):
@@ -156,8 +163,8 @@
                 parts = parted(later)
                 dk = dk + times_transposed(v, parts)
                 dv = dv + times(k, parts)
-            dk_ref[rows_of(b), j * HD:(j + 1) * HD] = dk
-            dv_ref[rows_of(b), j * HD:(j + 1) * HD] = dv
+            dk_ref[rows_of(b), j * HD:(j + 1) * HD] = dk.astype(jnp.bfloat16)
+            dv_ref[rows_of(b), j * HD:(j + 1) * HD] = dv.astype(jnp.bfloat16)
             if b > 0:
                 qg = over_rows(q, g)
                 later = qg if later is None else later + qg
@@ -168,14 +175,14 @@
     count = length // BLOCK
     wide = pl.BlockSpec((None, length, NEAR_HEADS * HD), lambda i: (0, 0, i))
     flat = pl.BlockSpec((1, length), lambda i: (0, 0))
-    term = pl.BlockSpec((NEAR_HEADS, 8, BLOCK), lambda i: (i, 0, 0))
+    term = pl.BlockSpec((TILE, HD), lambda i: (0, 0))
     return pl.pallas_call(
         functools.partial(kernel, count),
         grid=(H // NEAR_HEADS,),
         in_specs=[wide] * 4 + [flat] * 2,
         out_specs=[wide] * outputs + [term] * terms,
-        out_shape=[jax.ShapeDtypeStruct((1, length, features), jnp.float32)] * outputs
-        + [jax.ShapeDtypeStruct((H, 8, BLOCK), jnp.float32)] * terms,
+        out_shape=[jax.ShapeDtypeStruct((1, length, features), jnp.bfloat16)] * outputs
+        + [jax.ShapeDtypeStruct((TILE, HD), jnp.float32)] * terms,
         scratch_shapes=[pltpu.VMEM((count, BLOCK, BLOCK), jnp.float32)],
         compiler_params=params(FULL),
         cost_estimate=cost(28 * length * H * HD * HD, 20 * length * H * HD),
@@ -183,39 +190,57 @@
     )(*inputs, nodes, marks)
 
 
-def scan_kernel(spot_ref, own_ref, local_ref, out_ref):
+def scan_kernel(spot_ref, own_ref, local_ref, out_ref, held, gained, sems, sem):
     devices = own_ref.shape[0]
+    local = pltpu.make_async_copy(local_ref, gained, sem)
+    local.start()
+
+    def copy(at, late):
+        rows = slice(HD, 2 * HD + TILE) if late else slice(0, HD)
+        return pltpu.make_async_copy(held.at[at, rows], out_ref.at[at, rows], sems.at[at, late])
+
     total = jnp.zeros((HD, HD), jnp.float32)
     cross = jnp.zeros((HD, HD), jnp.float32)
     for at in range(devices):
-        out_ref[at, 0:HD] = total
+        held[at, 0:HD] = total
+        copy(at, 0).start()
         cross = cross + total * own_ref[at, HD:2 * HD]
         total = total + own_ref[at, 0:HD]
+    lanes = lax.broadcasted_iota(jnp.int32, (TILE, HD), 1)
+    local.wait()
+    terms = gained[...] + jnp.where(lanes == spot_ref[0], summed(cross), 0.0)
     total = jnp.zeros((HD, HD), jnp.float32)
     for at in reversed(range(devices)):
-        out_ref[at, HD:2 * HD] = total
+        held[at, HD:2 * HD] = total
+        held[at, 2 * HD:2 * HD + TILE] = terms
+        copy(at, 1).start()
         total = total + own_ref[at, HD:2 * HD]
-    cross = jnp.sum(jnp.sum(cross, axis=0, keepdims=True), axis=1, keepdims=True)
-    lanes = lax.broadcasted_iota(jnp.int32, (TILE, HD), 1)
-    terms = local_ref[...] + jnp.where(lanes == spot_ref[0], cross, 0.0)
     for at in range(devices):
-        out_ref[at, 2 * HD:2 * HD + TILE] = terms
+        for late in range(2):
+            copy(at, late).wait()
 
 
 def scan(spot, own, local):
     whole = pl.BlockSpec(memory_space=pltpu.VMEM)
+    shape = (own.shape[0], 2 * HD + TILE, HD)
     return pl.pallas_call(
         scan_kernel,
-        in_specs=[pl.BlockSpec(memory_space=pltpu.SMEM), whole, whole],
-        out_specs=whole,
-        out_shape=jax.ShapeDtypeStruct((own.shape[0], 2 * HD + TILE, HD), jnp.float32),
-        compiler_params=params(FULL),
+        in_specs=[pl.BlockSpec(memory_space=pltpu.SMEM), whole, pl.BlockSpec(memory_space=pltpu.HBM)],
+        out_specs=pl.BlockSpec(memory_space=pltpu.HBM),
+        out_shape=pltpu.HBM(shape, jnp.float32),
+        scratch_shapes=[
+            pltpu.VMEM(shape, jnp.float32),
+            pltpu.VMEM((TILE, HD), jnp.float32),
+            pltpu.SemaphoreType.DMA((own.shape[0], 2)),
+            pltpu.SemaphoreType.DMA,
+        ],
+        compiler_params=params(12 << 20),
         cost_estimate=cost(3 * own.size, 8 * own.size),
         name="scan",
-    )(spot, own, local)
-
-
-FAR_HEADS = 2
+    )(spot, own, pltpu.with_memory_space_constraint(local, pltpu.HBM))
+
+
+FAR_HEADS = 4
 
 
 def far_kernel(scale, gain_ref, k_ref, v_ref, g_ref, part_q_ref, part_k_ref, part_v_ref, state_ref,
@@ -223,8 +248,9 @@
     for j in range(FAR_HEADS):
         columns = slice(j * HD, (j + 1) * HD)
         factor = gain_ref[pl.program_id(0) * FAR_HEADS + j] * scale
-        prior = parted(state_ref[j, 0:HD])
-        later = parted(state_ref[j, HD:2 * HD])
+        at = pl.program_id(0) * FAR_HEADS + j
+        prior = parted(state_ref[at, 0:HD])
+        later = parted(state_ref[at, HD:2 * HD])
         dq = part_q_ref[:, columns] + times_transposed(g_ref[:, columns], prior)
         dq_ref[:, columns] = (dq * factor).astype(jnp.bfloat16)
         dk = part_k_ref[:, columns] + times_transposed(v_ref[:, columns], later)
@@ -236,14 +262,15 @@
 def far(scale, gain, k, v, g, parts, states):
     _, length, features = k.shape
     wide = pl.BlockSpec((None, length, FAR_HEADS * HD), lambda i: (0, 0, i))
-    state = pl.BlockSpec((FAR_HEADS, 2 * HD, HD), lambda i: (i, 0, 0))
+    state = pl.BlockSpec(memory_space=pltpu.VMEM)
+    k, v, g, *parts = (pltpu.with_memory_space_constraint(x, pltpu.HBM) for x in (k, v, g, *parts))
     return pl.pallas_call(
         functools.partial(far_kernel, scale),
         grid=(H // FAR_HEADS,),
         in_specs=[pl.BlockSpec(memory_space=pltpu.SMEM)] + [wide] * 6 + [state],
         out_specs=[wide] * 3,
         out_shape=[jax.ShapeDtypeStruct((1, length, features), jnp.bfloat16)] * 3,
-        compiler_params=params(FULL),
+        compiler_params=params(40 << 20),
         cost_estimate=cost(12 * length * H * HD * HD, 24 * length * H * HD),
         name="far",
     )(gain, k, v, g, *parts, states)
@@ -260,10 +287,9 @@
 
     inputs = (queries, keys, values, grad_out)
     owned = exchange(own_states(*inputs), "ctx")
-    part_q, own_term = near(near_q_kernel, inputs, node_ids, flags, 1, 1, "near_q")
+    part_q, local = near(near_q_kernel, inputs, node_ids, flags, 1, 1, "near_q")
     part_k, part_v = near(near_kv_kernel, inputs, node_ids, flags, 2, 0, "near_kv")
-    local = jnp.pad(jnp.sum(own_term, axis=(1, 2)), (0, HD - H))[None]
-    states = exchange(scan(spot, owned, jnp.broadcast_to(local, (TILE, HD))), "ctx")
+    states = exchange(scan(spot, owned, local), "ctx")
 
     terms = jnp.sum(states[:, 2 * HD:, :], axis=0)
     terms = exchange(jnp.broadcast_to(terms, (lax.axis_size("dp"), TILE, HD)), "dp")

time: 111 us -> 104 us (0.937)
  Pallas kernels: 75.4 us -> 65.1 us
  waiting for transfers between devices: 10.6 us -> 16.5 us
  local copies, waits for them, and re-layouts: 2.01 us -> 0.62 us
    all_to_all x3, waiting for transfers between devices: 10.6 us -> 16.5 us  [exchange(): return lax.all_to_all(block, axis, 0, 0, tiled=True)]
    pallas_call x2, Pallas kernels: 48.9 us -> 44 us  [near(): pl.pallas_call(functools.partial(kernel, count), grid=(H // NEAR_HEADS,),...]
    pallas_call x1, Pallas kernels: 15.9 us -> 11.9 us  [far(): pl.pallas_call(functools.partial(far_kernel, scale), grid=(H // FAR_HEADS...]
    pallas_call x1, Pallas kernels: 3.21 us -> 2.1 us  [scan(): pl.pallas_call(scan_kernel, in_specs=[pl.BlockSpec(memory_space=pltpu.SME...]
  transfers between devices with their start and end apart: 3 -> 3, of which waited for: 2 -> 2; matrix products, arithmetic and copies ran while one was open for 1% -> 0% of each run, Pallas kernels for 59% -> 54%
where the time goes in v2:
time: 104 us; the launch traced here: 103 us
  Pallas kernels  65.1 us (63%)
  starting transfers between devices  19.8 us (19%)
  waiting for transfers between devices  16.5 us (16%)
    pallas_call x2, Pallas kernels, near(): pl.pallas_call(functools.partial(kernel, count), grid=(H // NEAR_HEADS,),...  44 us
    all_to_all x3, starting transfers between devices, exchange(): return lax.all_to_all(block, axis, 0, 0, tiled=True)  19.8 us
    all_to_all x3, waiting for transfers between devices, exchange(): return lax.all_to_all(block, axis, 0, 0, tiled=True)  16.5 us
    pallas_call x1, Pallas kernels, far(): pl.pallas_call(functools.partial(far_kernel, scale), grid=(H // FAR_HEADS...  11.9 us
    pallas_call x1, Pallas kernels, own_states(): pl.pallas_call(state_kernel, in_specs=[pl.BlockSpec(memory_space=pltpu.HB...  7.03 us
    pallas_call x1, Pallas kernels, scan(): pl.pallas_call(scan_kernel, in_specs=[pl.BlockSpec(memory_space=pltpu.SME...  2.1 us
  transfers between devices with their start and end apart: 3, of which 2 were waited for; matrix products, arithmetic and copies ran while one was open for 0% of the time, Pallas kernels for 54%

profile of v2, /device:TPU:1, one launch (start us, length us, event | category | flops | bytes accessed | tf_op | source)
XLA Modules:
  0.0 103.2 jit_solution(4477276930074309817)
XLA Ops:
  0.6 7.0 %own_states.1 = f32[16,256,128]{2,1,0:T(8,128)} custom-call(bf16[1,768,2048]{2,1,0:T(8,128)(2,1)} %refs_0_.1, bf16[1,768,2048]{2,1,0:T(8,128)(2,1)} %k_ref.5, bf16[1,768,2048]{2,1,0:T(8,128)(2,1)} %v_ref.5, bf16[1,768,2048]{2,1,0:T(8,128)(2,1)} %g_ref.5), custom_call_target="tpu_custom_call" | custom-call | flops 805306368 | bytes 12582912 | tf_op jit(solution)/shard_map/own_states/pallas_call | solution.py:89
  7.7 8.4 %all-to-all-start = ((f32[16,256,128]{2,1,0:T(8,128)}), f32[16,256,128]{2,1,0:T(8,128)S(1)}, u32[]{:S(2)}, u32[]{:S(2)}) async-start(f32[16,256,128]{2,1,0:T(8,128)} %own_states.1), calls=%async_computation | async-start | bytes 4194304 | tf_op jit(solution)/shard_map/all_to_all | solution.py:280
  16.1 19.8 %near_q.1 = (bf16[1,768,2048]{2,1,0:T(8,128)(2,1)}, f32[8,128]{1,0:T(8,128)}) custom-call(bf16[1,768,2048]{2,1,0:T(8,128)(2,1)} %refs_0_.1, bf16[1,768,2048]{2,1,0:T(8,128)(2,1)} %k_ref.5, bf16[1,768,2048]{2,1,0:T(8,128)(2,1)} %v_ref.5, bf16[1,768,2048]{2,1,0:T(8,128)(2,1)} %g_ref.5, s32[1,768]{1,0:T(1,128)} %nodes_ref.3, s32[1,768]{1,0:T(1,128)} %marks_ref.3), custom_call_target="tpu_custom_call" | custom-call | flops 5637144576 | bytes 31457280 | tf_op jit(solution)/shard_map/near_q/pallas_call | solution.py:179
  35.9 11.2 %all-to-all-done.own_ref = f32[16,256,128]{2,1,0:T(8,128)S(1)} async-done(((f32[16,256,128]{2,1,0:T(8,128)}), f32[16,256,128]{2,1,0:T(8,128)S(1)}, u32[]{:S(2)}, u32[]{:S(2)}) %all-to-all-start) | async-done | bytes 2097184 | tf_op jit(solution)/shard_map/all_to_all | solution.py:280
  47.1 2.1 %scan.1 = f32[16,264,128]{2,1,0:T(8,128)} custom-call(s32[1]{0:T(128)} %bitcast.spot_ref, f32[16,256,128]{2,1,0:T(8,128)S(1)} %all-to-all-done.own_ref, f32[8,128]{1,0:T(8,128)} %get-tuple-element.14.local_ref), custom_call_target="tpu_custom_call" | custom-call | flops 1572864 | bytes 4194304 | tf_op jit(solution)/shard_map/scan/pallas_call | solution.py:226
  49.2 3.8 %all-to-all-start.1 = ((f32[16,264,128]{2,1,0:T(8,128)}), f32[16,264,128]{2,1,0:T(8,128)S(1)}, u32[]{:S(2)}, u32[]{:S(2)}) async-start(f32[16,264,128]{2,1,0:T(8,128)} %scan.1), calls=%async_computation.1 | async-start | bytes 4325376 | tf_op jit(solution)/shard_map/all_to_all | solution.py:280
  53.0 0.0 copy-start
  53.0 24.2 %near_kv.1 = (bf16[1,768,2048]{2,1,0:T(8,128)(2,1)}, bf16[1,768,2048]{2,1,0:T(8,128)(2,1)}) custom-call(bf16[1,768,2048]{2,1,0:T(8,128)(2,1)} %refs_0_.1, bf16[1,768,2048]{2,1,0:T(8,128)(2,1)} %k_ref.5, bf16[1,768,2048]{2,1,0:T(8,128)(2,1)} %v_ref.5, bf16[1,768,2048]{2,1,0:T(8,128)(2,1)} %g_ref.5, s32[1,768]{1,0:T(1,128)} %nodes_ref.3, s32[1,768]{1,0:T(1,128)} %marks_ref.3), custom_call_target="tpu_custom_call" | custom-call | flops 5637144576 | bytes 31457280 | tf_op jit(solution)/shard_map/near_kv/pallas_call | solution.py:179
  77.3 5.3 %all-to-all-done.1.state_ref = f32[16,264,128]{2,1,0:T(8,128)S(1)} async-done(((f32[16,264,128]{2,1,0:T(8,128)}), f32[16,264,128]{2,1,0:T(8,128)S(1)}, u32[]{:S(2)}, u32[]{:S(2)}) %all-to-all-start.1) | async-done | bytes 2162720 | tf_op jit(solution)/shard_map/all_to_all | solution.py:280
  82.6 0.6 broadcast_in_dim.7
  83.2 7.5 %all-to-all-start.2 = ((f32[8,8,128]{2,1,0:T(8,128)}), f32[8,8,128]{2,1,0:T(8,128)S(1)}, u32[]{:S(2)}, u32[]{:S(2)}) async-start(f32[8,8,128]{2,1,0:T(8,128)} %broadcast_in_dim.7), calls=%async_computation.2 | async-start | bytes 65536 | tf_op jit(solution)/shard_map/all_to_all | solution.py:280
  90.7 0.0 copy-done
  90.7 11.9 %far.1 = (bf16[1,768,2048]{2,1,0:T(8,128)(2,1)}, bf16[1,768,2048]{2,1,0:T(8,128)(2,1)}, bf16[1,768,2048]{2,1,0:T(8,128)(2,1)}) custom-call(f32[16]{0:T(128)S(1)} %copy-done, bf16[1,768,2048]{2,1,0:T(8,128)(2,1)} %k_ref.5, bf16[1,768,2048]{2,1,0:T(8,128)(2,1)} %v_ref.5, bf16[1,768,2048]{2,1,0:T(8,128)(2,1)} %g_ref.5, ...), custom_call_target="tpu_custom_call" | custom-call | flops 2415919104 | bytes 37748736 | tf_op jit(solution)/shard_map/far/pallas_call | solution.py:267
  102.7 0.0 all-to-all-done.2
  102.7 0.5 multiply_bitcast_fusion
  (2 shorter events, 0.0 us)
Async XLA Ops:
  7.7 39.4 %all-to-all-start = ((f32[16,256,128]{2,1,0:T(8,128)}), f32[16,256,128]{2,1,0:T(8,128)S(1)}, u32[]{:S(2)}, u32[]{:S(2)}) async-start(f32[16,256,128]{2,1,0:T(8,128)} %own_states.1), calls=%async_computation | async-start | bytes 4194304 | tf_op jit(solution)/shard_map/all_to_all | solution.py:280
  49.2 33.4 %all-to-all-start.1 = ((f32[16,264,128]{2,1,0:T(8,128)}), f32[16,264,128]{2,1,0:T(8,128)S(1)}, u32[]{:S(2)}, u32[]{:S(2)}) async-start(f32[16,264,128]{2,1,0:T(8,128)} %scan.1), calls=%async_computation.1 | async-start | bytes 4325376 | tf_op jit(solution)/shard_map/all_to_all | solution.py:280
  53.0 37.7 %copy-start = (f32[16]{0:T(128)S(1)}, f32[16]{0:T(128)}, u32[]{:S(2)}) copy-start(f32[16]{0:T(128)} %gain_ref.1) | copy-start | bytes 196
  83.2 19.4 %all-to-all-start.2 = ((f32[8,8,128]{2,1,0:T(8,128)}), f32[8,8,128]{2,1,0:T(8,128)S(1)}, u32[]{:S(2)}, u32[]{:S(2)}) async-start(f32[8,8,128]{2,1,0:T(8,128)} %broadcast_in_dim.7), calls=%async_computation.2 | async-start | bytes 65536 | tf_op jit(solution)/shard_map/all_to_all | solution.py:280

commit v3 on v2

--- a/solution.py
+++ b/solution.py
@@ -118,75 +118,81 @@
     return ((cols <= rows) & ((across == across.T) | (marks == 1))).astype(jnp.float32)
 
 
-def near_q_kernel(count, q_ref, k_ref, v_ref, g_ref, nodes_ref, marks_ref, dq_ref, term_ref, seen_ref):
+def near_kernel(count, q_ref, k_ref, v_ref, g_ref, nodes_ref, marks_ref,
+                dq_ref, dk_ref, dv_ref, term_ref, seen_ref, turned_ref, earlier_ref):
     @pl.when(pl.program_id(0) == 0)
     def _():
         for b in range(count):
             seen_ref[b] = visible(nodes_ref, marks_ref, b)
+            turned_ref[b] = visible(nodes_ref, marks_ref, b).T
         term_ref[...] = jnp.zeros_like(term_ref)
 
-    for j in range(NEAR_HEADS):
-        term = jnp.zeros((BLOCK, BLOCK), jnp.float32)
-        earlier = None
-        for b in range(count):
-            q, k, v, g = (head(ref, j, rows_of(b)) for ref in (q_ref, k_ref, v_ref, g_ref))
-            seen = seen_ref[b]
-            dscores = over_cols(g, v) * seen
-            term = term + over_cols(q, k) * dscores
-            dq = plain(dscores.astype(jnp.bfloat16), k)
-            if earlier is not None:
-                term = term + earlier * over_rows(q, g)
-                dq = dq + times_transposed(g, parted(earlier))
-            dq_ref[rows_of(b), j * HD:(j + 1) * HD] = dq.astype(jnp.bfloat16)
-            if b < count - 1:
-                kv = over_rows(k, v)
-                earlier = kv if earlier is None else earlier + kv
-        lanes = lax.broadcasted_iota(jnp.int32, (TILE, HD), 1)
+    heads = range(NEAR_HEADS)
+
+    def loaded(ref, b):
+        return [head(ref, j, rows_of(b)) for j in heads]
+
+    def store(ref, b, values):
+        for j in heads:
+            ref[rows_of(b), j * HD:(j + 1) * HD] = values[j].astype(jnp.bfloat16)
+
+    earlier = None
+    for b in range(count):
+        k, v, g = (loaded(ref, b) for ref in (k_ref, v_ref, g_ref))
+        dscores = [(over_cols(g[j], v[j]) * seen_ref[b]).astype(jnp.bfloat16) for j in heads]
+        kv = [over_rows(k[j], v[j]) for j in heads] if b < count - 1 else None
+        dq = [plain(dscores[j], k[j]) for j in heads]
+        if earlier is not None:
+            dq = [dq[j] + times_transposed(g[j], parted(earlier[j])) for j in heads]
+            for j in heads:
+                earlier_ref[j, b] = earlier[j]
+        store(dq_ref, b, dq)
+        if kv is not None:
+            earlier = kv if earlier is None else [earlier[j] + kv[j] for j in heads]
+
+    later = None
+    term = [jnp.zeros((BLOCK, BLOCK), jnp.float32) for j in heads]
+    for b in reversed(range(count)):
+        q, k, v, g = (loaded(ref, b) for ref in (q_ref, k_ref, v_ref, g_ref))
+        scores = [over_cols(k[j], q[j]) * turned_ref[b] for j in heads]
+        dscores = [over_cols(v[j], g[j]) * turned_ref[b] for j in heads]
+        qg = [over_rows(q[j], g[j]) for j in heads] if b > 0 else None
+        term = [term[j] + scores[j] * dscores[j] for j in heads]
+        dk = [plain(dscores[j].astype(jnp.bfloat16), q[j]) for j in heads]
+        dv = [plain(scores[j].astype(jnp.bfloat16), g[j]) for j in heads]
+        if later is not None:
+            parts = [parted(later[j]) for j in heads]
+            dk = [dk[j] + times_transposed(v[j], parts[j]) for j in heads]
+            dv = [dv[j] + times(k[j], parts[j]) for j in heads]
+        store(dk_ref, b, dk)
+        store(dv_ref, b, dv)
+        if qg is not None:
+            term = [term[j] + earlier_ref[j, b] * qg[j] for j in heads]
+            later = qg if later is None else [later[j] + qg[j] for j in heads]
+
+    lanes = lax.broadcasted_iota(jnp.int32, (TILE, HD), 1)
+    for j in heads:
         here = lanes == pl.program_id(0) * NEAR_HEADS + j
-        term_ref[...] += jnp.where(here, summed(term), 0.0)
-
-
-def near_kv_kernel(count, q_ref, k_ref, v_ref, g_ref, nodes_ref, marks_ref, dk_ref, dv_ref, seen_ref):
-    @pl.when(pl.program_id(0) == 0)
-    def _():
-        for b in range(count):
-            seen_ref[b] = visible(nodes_ref, marks_ref, b).T
-
-    for j in range(NEAR_HEADS):
-        later = None
-        for b in reversed(range(count)):
-            q, k, v, g = (head(ref, j, rows_of(b)) for ref in (q_ref, k_ref, v_ref, g_ref))
-            seen = seen_ref[b]
-            dk = plain((over_cols(v, g) * seen).astype(jnp.bfloat16), q)
-            dv = plain((over_cols(k, q) * seen).astype(jnp.bfloat16), g)
-            if later is not None:
-                parts = parted(later)
-                dk = dk + times_transposed(v, parts)
-                dv = dv + times(k, parts)
-            dk_ref[rows_of(b), j * HD:(j + 1) * HD] = dk.astype(jnp.bfloat16)
-            dv_ref[rows_of(b), j * HD:(j + 1) * HD] = dv.astype(jnp.bfloat16)
-            if b > 0:
-                qg = over_rows(q, g)
-                later = qg if later is None else later + qg
-
-
-def near(kernel, inputs, nodes, marks, outputs, terms, name):
+        term_ref[...] += jnp.where(here, summed(term[j]), 0.0)
+
+
+def near(inputs, nodes, marks):
     _, length, features = inputs[0].shape
     count = length // BLOCK
     wide = pl.BlockSpec((None, length, NEAR_HEADS * HD), lambda i: (0, 0, i))
     flat = pl.BlockSpec((1, length), lambda i: (0, 0))
-    term = pl.BlockSpec((TILE, HD), lambda i: (0, 0))
+    masks = pltpu.VMEM((count, BLOCK, BLOCK), jnp.float32)
     return pl.pallas_call(
-        functools.partial(kernel, count),
+        functools.partial(near_kernel, count),
         grid=(H // NEAR_HEADS,),
         in_specs=[wide] * 4 + [flat] * 2,
-        out_specs=[wide] * outputs + [term] * terms,
-        out_shape=[jax.ShapeDtypeStruct((1, length, features), jnp.bfloat16)] * outputs
-        + [jax.ShapeDtypeStruct((TILE, HD), jnp.float32)] * terms,
-        scratch_shapes=[pltpu.VMEM((count, BLOCK, BLOCK), jnp.float32)],
+        out_specs=[wide] * 3 + [pl.BlockSpec((TILE, HD), lambda i: (0, 0))],
+        out_shape=[jax.ShapeDtypeStruct((1, length, features), jnp.bfloat16)] * 3
+        + [jax.ShapeDtypeStruct((TILE, HD), jnp.float32)],
+        scratch_shapes=[masks, masks, pltpu.VMEM((NEAR_HEADS, count, BLOCK, BLOCK), jnp.float32)],
         compiler_params=params(FULL),
-        cost_estimate=cost(28 * length * H * HD * HD, 20 * length * H * HD),
-        name=name,
+        cost_estimate=cost(28 * length * H * HD * HD, 14 * length * H * HD),
+        name="near",
     )(*inputs, nodes, marks)
 
 
@@ -287,8 +293,7 @@
 
     inputs = (queries, keys, values, grad_out)
     owned = exchange(own_states(*inputs), "ctx")
-    part_q, local = near(near_q_kernel, inputs, node_ids, flags, 1, 1, "near_q")
-    part_k, part_v = near(near_kv_kernel, inputs, node_ids, flags, 2, 0, "near_kv")
+    *parts, local = near(inputs, node_ids, flags)
     states = exchange(scan(spot, owned, local), "ctx")
 
     terms = jnp.sum(states[:, 2 * HD:, :], axis=0)
@@ -296,7 +301,7 @@
     norm_tokens = lax.axis_size("dp") * length * lax.axis_size("ctx") * HD
     grad_gain = jnp.sum(terms, axis=0)[0, :H] * scale / math.sqrt(norm_tokens)
 
-    return (*far(scale, gain, keys, values, grad_out, (part_q, part_k, part_v), states), grad_gain)
+    return (*far(scale, gain, keys, values, grad_out, parts, states), grad_gain)
 
 
 def solution(mesh):

time: 104 us -> 101 us (0.971)
  blocking collectives: 0 us -> 31.6 us
  Pallas kernels: 65.1 us -> 48.1 us
  waiting for transfers between devices: 16.5 us -> 3.96 us
  starting transfers between devices: 19.8 us -> 15.3 us
    all_to_all x0 -> x1, blocking collectives: none -> 31.6 us  [exchange(): return lax.all_to_all(block, axis, 0, 0, tiled=True)]
    pallas_call x2 -> x1, Pallas kernels: 44 us -> 27 us  [near(): pl.pallas_call(functools.partial(near_kernel, count), grid=(H // NEAR_HEA...]
    all_to_all x3 -> x2, waiting for transfers between devices: 16.5 us -> 3.96 us  [exchange(): return lax.all_to_all(block, axis, 0, 0, tiled=True)]
    all_to_all x3 -> x2, starting transfers between devices: 19.8 us -> 15.3 us  [exchange(): return lax.all_to_all(block, axis, 0, 0, tiled=True)]
  transfers between devices with their start and end apart: 3 -> 2, of which waited for: 2 -> 1; matrix products, arithmetic and copies ran while one was open for 0% -> 0% of each run, Pallas kernels for 54% -> 39%
where the time goes in v3:
time: 101 us
  Pallas kernels  48.1 us (48%)
  blocking collectives  31.6 us (31%)
  starting transfers between devices  15.3 us (15%)
  waiting for transfers between devices  3.96 us (4%)
    all_to_all x1, blocking collectives, exchange(): return lax.all_to_all(block, axis, 0, 0, tiled=True)  31.6 us
    pallas_call x1, Pallas kernels, near(): pl.pallas_call(functools.partial(near_kernel, count), grid=(H // NEAR_HEA...  27 us
    all_to_all x2, starting transfers between devices, exchange(): return lax.all_to_all(block, axis, 0, 0, tiled=True)  15.3 us
    pallas_call x1, Pallas kernels, far(): pl.pallas_call(functools.partial(far_kernel, scale), grid=(H // FAR_HEADS...  11.9 us
    pallas_call x1, Pallas kernels, own_states(): pl.pallas_call(state_kernel, in_specs=[pl.BlockSpec(memory_space=pltpu.HB...  7.03 us
    all_to_all x2, waiting for transfers between devices, exchange(): return lax.all_to_all(block, axis, 0, 0, tiled=True)  3.96 us
    pallas_call x1, Pallas kernels, scan(): pl.pallas_call(scan_kernel, in_specs=[pl.BlockSpec(memory_space=pltpu.SME...  2.1 us
  transfers between devices with their start and end apart: 2, of which 1 were waited for; matrix products, arithmetic and copies ran while one was open for 0% of the time, Pallas kernels for 39%

profile of v3, /device:TPU:1, one launch (start us, length us, event | category | flops | bytes accessed | tf_op | source)
XLA Modules:
  0.0 100.8 jit_solution(3539241325333079755)
XLA Ops:
  0.6 7.0 %own_states.1 = f32[16,256,128]{2,1,0:T(8,128)} custom-call(bf16[1,768,2048]{2,1,0:T(8,128)(2,1)} %refs_0_.1, bf16[1,768,2048]{2,1,0:T(8,128)(2,1)} %k_ref.3, bf16[1,768,2048]{2,1,0:T(8,128)(2,1)} %v_ref.3, bf16[1,768,2048]{2,1,0:T(8,128)(2,1)} %g_ref.3), custom_call_target="tpu_custom_call" | custom-call | flops 805306368 | bytes 12582912 | tf_op jit(solution)/shard_map/own_states/pallas_call | solution.py:89
  7.7 8.4 %all-to-all-start = ((f32[16,256,128]{2,1,0:T(8,128)}), f32[16,256,128]{2,1,0:T(8,128)S(1)}, u32[]{:S(2)}, u32[]{:S(2)}) async-start(f32[16,256,128]{2,1,0:T(8,128)} %own_states.1), calls=%async_computation | async-start | bytes 4194304 | tf_op jit(solution)/shard_map/all_to_all | solution.py:286
  16.1 27.0 %near.1 = (bf16[1,768,2048]{2,1,0:T(8,128)(2,1)}, bf16[1,768,2048]{2,1,0:T(8,128)(2,1)}, bf16[1,768,2048]{2,1,0:T(8,128)(2,1)}, f32[8,128]{1,0:T(8,128)}) custom-call(bf16[1,768,2048]{2,1,0:T(8,128)(2,1)} %refs_0_.1, bf16[1,768,2048]{2,1,0:T(8,128)(2,1)} %k_ref.3, bf16[1,768,2048]{2,1,0:T(8,128)(2,1)} %v_ref.3, bf16[1,768,2048]{2,1,0:T(8,128)(2,1)} %g_ref.3, ...), custom_call_target="tpu_custom_call" | custom-call | flops 5637144576 | bytes 22020096 | tf_op jit(solution)/shard_map/near/pallas_call | solution.py:185
  43.1 4.0 %all-to-all-done.own_ref = f32[16,256,128]{2,1,0:T(8,128)S(1)} async-done(((f32[16,256,128]{2,1,0:T(8,128)}), f32[16,256,128]{2,1,0:T(8,128)S(1)}, u32[]{:S(2)}, u32[]{:S(2)}) %all-to-all-start) | async-done | bytes 2097184 | tf_op jit(solution)/shard_map/all_to_all | solution.py:286
  47.1 2.1 %scan.1 = f32[16,264,128]{2,1,0:T(8,128)} custom-call(s32[1]{0:T(128)} %bitcast.spot_ref, f32[16,256,128]{2,1,0:T(8,128)S(1)} %all-to-all-done.own_ref, f32[8,128]{1,0:T(8,128)} %get-tuple-element.14.local_ref), custom_call_target="tpu_custom_call" | custom-call | flops 1572864 | bytes 4194304 | tf_op jit(solution)/shard_map/scan/pallas_call | solution.py:232
  49.2 0.0 copy-start
  49.2 31.6 %all_to_all.15.state_ref = f32[16,264,128]{2,1,0:T(8,128)S(1)} all-to-all(f32[16,264,128]{2,1,0:T(8,128)} %scan.1), channel_id=1, replica_groups=mesh['dp'=8,'ctx'=16] {'ctx'}, dimensions={0} | all-to-all | bytes 4325376 | tf_op jit(solution)/shard_map/all_to_all | solution.py:286
  80.8 0.6 broadcast_in_dim.7
  81.4 6.9 %all-to-all-start.2 = ((f32[8,8,128]{2,1,0:T(8,128)}), f32[8,8,128]{2,1,0:T(8,128)S(1)}, u32[]{:S(2)}, u32[]{:S(2)}) async-start(f32[8,8,128]{2,1,0:T(8,128)} %broadcast_in_dim.7), calls=%async_computation.2 | async-start | bytes 65536 | tf_op jit(solution)/shard_map/all_to_all | solution.py:286
  88.3 0.0 copy-done
  88.3 11.9 %far.1 = (bf16[1,768,2048]{2,1,0:T(8,128)(2,1)}, bf16[1,768,2048]{2,1,0:T(8,128)(2,1)}, bf16[1,768,2048]{2,1,0:T(8,128)(2,1)}) custom-call(f32[16]{0:T(128)S(1)} %copy-done, bf16[1,768,2048]{2,1,0:T(8,128)(2,1)} %k_ref.3, bf16[1,768,2048]{2,1,0:T(8,128)(2,1)} %v_ref.3, bf16[1,768,2048]{2,1,0:T(8,128)(2,1)} %g_ref.3, ...), custom_call_target="tpu_custom_call" | custom-call | flops 2415919104 | bytes 37748736 | tf_op jit(solution)/shard_map/far/pallas_call | solution.py:273
  100.2 0.0 all-to-all-done.2
  100.3 0.5 multiply_bitcast_fusion
  (2 shorter events, 0.0 us)
Async XLA Ops:
  7.7 39.4 %all-to-all-start = ((f32[16,256,128]{2,1,0:T(8,128)}), f32[16,256,128]{2,1,0:T(8,128)S(1)}, u32[]{:S(2)}, u32[]{:S(2)}) async-start(f32[16,256,128]{2,1,0:T(8,128)} %own_states.1), calls=%async_computation | async-start | bytes 4194304 | tf_op jit(solution)/shard_map/all_to_all | solution.py:286
  49.2 39.1 %copy-start = (f32[16]{0:T(128)S(1)}, f32[16]{0:T(128)}, u32[]{:S(2)}) copy-start(f32[16]{0:T(128)} %gain_ref.1) | copy-start | bytes 196
  81.4 18.8 %all-to-all-start.2 = ((f32[8,8,128]{2,1,0:T(8,128)}), f32[8,8,128]{2,1,0:T(8,128)S(1)}, u32[]{:S(2)}, u32[]{:S(2)}) async-start(f32[8,8,128]{2,1,0:T(8,128)} %broadcast_in_dim.7), calls=%async_computation.2 | async-start | bytes 65536 | tf_op jit(solution)/shard_map/all_to_all | solution.py:286

commit v4 on v3

--- a/solution.py
+++ b/solution.py
@@ -58,11 +58,11 @@
     return pltpu.CompilerParams(vmem_limit_bytes=vmem)
 
 
-CHUNKS = 4
+CHUNKS = 8
 
 
 def state_kernel(*refs):
-    sources, out_ref, kept, sems = refs[:4], refs[4], refs[5:9], refs[9]
+    sources, out_ref, kept, held, sems, out_sems = refs[:4], refs[4], refs[5:9], refs[9], refs[10], refs[11]
     wide = sources[0].shape[2] // CHUNKS
     heads = wide // HD
 
@@ -71,6 +71,10 @@
         return pltpu.make_async_copy(
             sources[i].at[0, :, columns], kept[i].at[:, columns], sems.at[i, n]
         )
+
+    def result(n):
+        part = slice(n * heads, (n + 1) * heads)
+        return pltpu.make_async_copy(held.at[part], out_ref.at[part], out_sems.at[n])
 
     for n in range(CHUNKS):
         for i in range(4):
@@ -80,8 +84,12 @@
             copy(i, n).wait()
         for j in range(n * heads, (n + 1) * heads):
             q, k, v, g = (head(ref, j) for ref in kept)
-            out_ref[j, 0:HD] = over_rows(k, v)
-            out_ref[j, HD:2 * HD] = over_rows(q, g)
+            both = over_rows(jnp.concatenate([k, q], axis=1), jnp.concatenate([v, g], axis=1))
+            held[j, 0:HD] = both[:HD, :HD]
+            held[j, HD:2 * HD] = both[HD:, HD:]
+        result(n).start()
+    for n in range(CHUNKS):
+        result(n).wait()
 
 
 def own_states(q, k, v, g):
@@ -89,10 +97,14 @@
     return pl.pallas_call(
         state_kernel,
         in_specs=[pl.BlockSpec(memory_space=pltpu.HBM)] * 4,
-        out_specs=pl.BlockSpec(memory_space=pltpu.VMEM),
-        out_shape=jax.ShapeDtypeStruct((H, 2 * HD, HD), jnp.float32),
+        out_specs=pl.BlockSpec(memory_space=pltpu.HBM),
+        out_shape=pltpu.HBM((H, 2 * HD, HD), jnp.float32),
         scratch_shapes=[pltpu.VMEM((length, features), jnp.bfloat16)] * 4
-        + [pltpu.SemaphoreType.DMA((4, CHUNKS))],
+        + [
+            pltpu.VMEM((H, 2 * HD, HD), jnp.float32),
+            pltpu.SemaphoreType.DMA((4, CHUNKS)),
+            pltpu.SemaphoreType.DMA((CHUNKS,)),
+        ],
         compiler_params=params(FULL),
         cost_estimate=cost(4 * length * H * HD * HD, 8 * length * H * HD),
         name="own_states",

time: 101 us -> 101 us (level)
  no operation moved by 1% of the time
where the time goes in v4:
time: 101 us; the launch traced here: 100 us
  Pallas kernels  47.8 us (47%)
  blocking collectives  31.6 us (31%)
  starting transfers between devices  15.3 us (15%)
  waiting for transfers between devices  3.97 us (4%)
    all_to_all x1, blocking collectives, exchange(): return lax.all_to_all(block, axis, 0, 0, tiled=True)  31.6 us
    pallas_call x1, Pallas kernels, near(): pl.pallas_call(functools.partial(near_kernel, count), grid=(H // NEAR_HEA...  27 us
    all_to_all x2, starting transfers between devices, exchange(): return lax.all_to_all(block, axis, 0, 0, tiled=True)  15.3 us
    pallas_call x1, Pallas kernels, far(): pl.pallas_call(functools.partial(far_kernel, scale), grid=(H // FAR_HEADS...  11.9 us
    pallas_call x1, Pallas kernels, own_states(): pl.pallas_call(state_kernel, in_specs=[pl.BlockSpec(memory_space=pltpu.HB...  6.73 us
    all_to_all x2, waiting for transfers between devices, exchange(): return lax.all_to_all(block, axis, 0, 0, tiled=True)  3.97 us
    pallas_call x1, Pallas kernels, scan(): pl.pallas_call(scan_kernel, in_specs=[pl.BlockSpec(memory_space=pltpu.SME...  2.1 us
  transfers between devices with their start and end apart: 2, of which 1 were waited for; matrix products, arithmetic and copies ran while one was open for 0% of the time, Pallas kernels for 39%

profile of v4, /device:TPU:1, one launch (start us, length us, event | category | flops | bytes accessed | tf_op | source)
XLA Modules:
  0.0 100.5 jit_solution(3459001041254688802)
XLA Ops:
  0.6 6.7 %own_states.1 = f32[16,256,128]{2,1,0:T(8,128)} custom-call(bf16[1,768,2048]{2,1,0:T(8,128)(2,1)} %refs_0_.1, bf16[1,768,2048]{2,1,0:T(8,128)(2,1)} %k_ref.3, bf16[1,768,2048]{2,1,0:T(8,128)(2,1)} %v_ref.3, bf16[1,768,2048]{2,1,0:T(8,128)(2,1)} %g_ref.3), custom_call_target="tpu_custom_call" | custom-call | flops 805306368 | bytes 12582912 | tf_op jit(solution)/shard_map/own_states/pallas_call | solution.py:97
  7.4 8.4 %all-to-all-start = ((f32[16,256,128]{2,1,0:T(8,128)}), f32[16,256,128]{2,1,0:T(8,128)S(1)}, u32[]{:S(2)}, u32[]{:S(2)}) async-start(f32[16,256,128]{2,1,0:T(8,128)} %own_states.1), calls=%async_computation | async-start | bytes 4194304 | tf_op jit(solution)/shard_map/all_to_all | solution.py:298
  15.8 27.0 %near.1 = (bf16[1,768,2048]{2,1,0:T(8,128)(2,1)}, bf16[1,768,2048]{2,1,0:T(8,128)(2,1)}, bf16[1,768,2048]{2,1,0:T(8,128)(2,1)}, f32[8,128]{1,0:T(8,128)}) custom-call(bf16[1,768,2048]{2,1,0:T(8,128)(2,1)} %refs_0_.1, bf16[1,768,2048]{2,1,0:T(8,128)(2,1)} %k_ref.3, bf16[1,768,2048]{2,1,0:T(8,128)(2,1)} %v_ref.3, bf16[1,768,2048]{2,1,0:T(8,128)(2,1)} %g_ref.3, ...), custom_call_target="tpu_custom_call" | custom-call | flops 5637144576 | bytes 22020096 | tf_op jit(solution)/shard_map/near/pallas_call | solution.py:197
  42.8 4.0 %all-to-all-done.own_ref = f32[16,256,128]{2,1,0:T(8,128)S(1)} async-done(((f32[16,256,128]{2,1,0:T(8,128)}), f32[16,256,128]{2,1,0:T(8,128)S(1)}, u32[]{:S(2)}, u32[]{:S(2)}) %all-to-all-start) | async-done | bytes 2097184 | tf_op jit(solution)/shard_map/all_to_all | solution.py:298
  46.8 2.1 %scan.1 = f32[16,264,128]{2,1,0:T(8,128)} custom-call(s32[1]{0:T(128)} %bitcast.spot_ref, f32[16,256,128]{2,1,0:T(8,128)S(1)} %all-to-all-done.own_ref, f32[8,128]{1,0:T(8,128)} %get-tuple-element.14.local_ref), custom_call_target="tpu_custom_call" | custom-call | flops 1572864 | bytes 4194304 | tf_op jit(solution)/shard_map/scan/pallas_call | solution.py:244
  48.9 0.0 copy-start
  48.9 31.6 %all_to_all.15.state_ref = f32[16,264,128]{2,1,0:T(8,128)S(1)} all-to-all(f32[16,264,128]{2,1,0:T(8,128)} %scan.1), channel_id=1, replica_groups=mesh['dp'=8,'ctx'=16] {'ctx'}, dimensions={0} | all-to-all | bytes 4325376 | tf_op jit(solution)/shard_map/all_to_all | solution.py:298
  80.5 0.6 broadcast_in_dim.7
  81.1 6.9 %all-to-all-start.2 = ((f32[8,8,128]{2,1,0:T(8,128)}), f32[8,8,128]{2,1,0:T(8,128)S(1)}, u32[]{:S(2)}, u32[]{:S(2)}) async-start(f32[8,8,128]{2,1,0:T(8,128)} %broadcast_in_dim.7), calls=%async_computation.2 | async-start | bytes 65536 | tf_op jit(solution)/shard_map/all_to_all | solution.py:298
  88.0 0.0 copy-done
  88.0 11.9 %far.1 = (bf16[1,768,2048]{2,1,0:T(8,128)(2,1)}, bf16[1,768,2048]{2,1,0:T(8,128)(2,1)}, bf16[1,768,2048]{2,1,0:T(8,128)(2,1)}) custom-call(f32[16]{0:T(128)S(1)} %copy-done, bf16[1,768,2048]{2,1,0:T(8,128)(2,1)} %k_ref.3, bf16[1,768,2048]{2,1,0:T(8,128)(2,1)} %v_ref.3, bf16[1,768,2048]{2,1,0:T(8,128)(2,1)} %g_ref.3, ...), custom_call_target="tpu_custom_call" | custom-call | flops 2415919104 | bytes 37748736 | tf_op jit(solution)/shard_map/far/pallas_call | solution.py:285
  99.9 0.0 all-to-all-done.2
  100.0 0.5 multiply_bitcast_fusion
  (2 shorter events, 0.0 us)
Async XLA Ops:
  7.4 39.4 %all-to-all-start = ((f32[16,256,128]{2,1,0:T(8,128)}), f32[16,256,128]{2,1,0:T(8,128)S(1)}, u32[]{:S(2)}, u32[]{:S(2)}) async-start(f32[16,256,128]{2,1,0:T(8,128)} %own_states.1), calls=%async_computation | async-start | bytes 4194304 | tf_op jit(solution)/shard_map/all_to_all | solution.py:298
  48.9 39.1 %copy-start = (f32[16]{0:T(128)S(1)}, f32[16]{0:T(128)}, u32[]{:S(2)}) copy-start(f32[16]{0:T(128)} %gain_ref.1) | copy-start | bytes 196
  81.1 18.8 %all-to-all-start.2 = ((f32[8,8,128]{2,1,0:T(8,128)}), f32[8,8,128]{2,1,0:T(8,128)S(1)}, u32[]{:S(2)}, u32[]{:S(2)}) async-start(f32[8,8,128]{2,1,0:T(8,128)} %broadcast_in_dim.7), calls=%async_computation.2 | async-start | bytes 65536 | tf_op jit(solution)/shard_map/all_to_all | solution.py:298

commit v5 on v4

--- a/solution.py
+++ b/solution.py
@@ -58,7 +58,7 @@
     return pltpu.CompilerParams(vmem_limit_bytes=vmem)
 
 
-CHUNKS = 8
+CHUNKS = 4
 
 
 def state_kernel(*refs):
@@ -294,6 +294,27 @@
     )(gain, k, v, g, *parts, states)
 
 
+def gathered_kernel(state_ref, out_ref):
+    total = state_ref[0, 2 * HD:2 * HD + TILE]
+    for at in range(1, state_ref.shape[0]):
+        total = total + state_ref[at, 2 * HD:2 * HD + TILE]
+    for at in range(out_ref.shape[0]):
+        out_ref[at] = total
+
+
+def gathered(states, copies):
+    whole = pl.BlockSpec(memory_space=pltpu.VMEM)
+    return pl.pallas_call(
+        gathered_kernel,
+        in_specs=[whole],
+        out_specs=whole,
+        out_shape=jax.ShapeDtypeStruct((copies, TILE, HD), jnp.float32),
+        compiler_params=params(4 << 20),
+        cost_estimate=cost(states.shape[0] * TILE * HD, 4 * copies * TILE * HD),
+        name="gathered",
+    )(states)
+
+
 def exchange(block, axis):
     return lax.all_to_all(block, axis, 0, 0, tiled=True)
 
@@ -308,8 +329,7 @@
     *parts, local = near(inputs, node_ids, flags)
     states = exchange(scan(spot, owned, local), "ctx")
 
-    terms = jnp.sum(states[:, 2 * HD:, :], axis=0)
-    terms = exchange(jnp.broadcast_to(terms, (lax.axis_size("dp"), TILE, HD)), "dp")
+    terms = exchange(gathered(states, lax.axis_size("dp")), "dp")
     norm_tokens = lax.axis_size("dp") * length * lax.axis_size("ctx") * HD
     grad_gain = jnp.sum(terms, axis=0)[0, :H] * scale / math.sqrt(norm_tokens)
 

time: 101 us -> 101 us (level)
  no operation moved by 1% of the time
where the time goes in v5:
time: 101 us; the launch traced here: 100 us
  Pallas kernels  48.4 us (48%)
  blocking collectives  31.6 us (31%)
  starting transfers between devices  15.3 us (15%)
  waiting for transfers between devices  3.96 us (4%)
    all_to_all x1, blocking collectives, exchange(): return lax.all_to_all(block, axis, 0, 0, tiled=True)  31.6 us
    pallas_call x1, Pallas kernels, near(): pl.pallas_call(functools.partial(near_kernel, count), grid=(H // NEAR_HEA...  27 us
    all_to_all x2, starting transfers between devices, exchange(): return lax.all_to_all(block, axis, 0, 0, tiled=True)  15.3 us
    pallas_call x1, Pallas kernels, far(): pl.pallas_call(functools.partial(far_kernel, scale), grid=(H // FAR_HEADS...  11.9 us
    pallas_call x1, Pallas kernels, own_states(): pl.pallas_call(state_kernel, in_specs=[pl.BlockSpec(memory_space=pltpu.HB...  6.7 us
    all_to_all x2, waiting for transfers between devices, exchange(): return lax.all_to_all(block, axis, 0, 0, tiled=True)  3.96 us
    pallas_call x1, Pallas kernels, scan(): pl.pallas_call(scan_kernel, in_specs=[pl.BlockSpec(memory_space=pltpu.SME...  2.1 us
  transfers between devices with their start and end apart: 2, of which 1 were waited for; matrix products, arithmetic and copies ran while one was open for 0% of the time, Pallas kernels for 39%

profile of v5, /device:TPU:1, one launch (start us, length us, event | category | flops | bytes accessed | tf_op | source)
XLA Modules:
  0.0 100.4 jit_solution(13440168328923396017)
XLA Ops:
  0.6 6.7 %own_states.1 = f32[16,256,128]{2,1,0:T(8,128)} custom-call(bf16[1,768,2048]{2,1,0:T(8,128)(2,1)} %refs_0_.1, bf16[1,768,2048]{2,1,0:T(8,128)(2,1)} %k_ref.3, bf16[1,768,2048]{2,1,0:T(8,128)(2,1)} %v_ref.3, bf16[1,768,2048]{2,1,0:T(8,128)(2,1)} %g_ref.3), custom_call_target="tpu_custom_call" | custom-call | flops 805306368 | bytes 12582912 | tf_op jit(solution)/shard_map/own_states/pallas_call | solution.py:97
  7.3 8.4 %all-to-all-start = ((f32[16,256,128]{2,1,0:T(8,128)}), f32[16,256,128]{2,1,0:T(8,128)S(1)}, u32[]{:S(2)}, u32[]{:S(2)}) async-start(f32[16,256,128]{2,1,0:T(8,128)} %own_states.1), calls=%async_computation | async-start | bytes 4194304 | tf_op jit(solution)/shard_map/all_to_all | solution.py:319
  15.8 27.0 %near.1 = (bf16[1,768,2048]{2,1,0:T(8,128)(2,1)}, bf16[1,768,2048]{2,1,0:T(8,128)(2,1)}, bf16[1,768,2048]{2,1,0:T(8,128)(2,1)}, f32[8,128]{1,0:T(8,128)}) custom-call(bf16[1,768,2048]{2,1,0:T(8,128)(2,1)} %refs_0_.1, bf16[1,768,2048]{2,1,0:T(8,128)(2,1)} %k_ref.3, bf16[1,768,2048]{2,1,0:T(8,128)(2,1)} %v_ref.3, bf16[1,768,2048]{2,1,0:T(8,128)(2,1)} %g_ref.3, ...), custom_call_target="tpu_custom_call" | custom-call | flops 5637144576 | bytes 22020096 | tf_op jit(solution)/shard_map/near/pallas_call | solution.py:197
  42.8 4.0 %all-to-all-done.own_ref = f32[16,256,128]{2,1,0:T(8,128)S(1)} async-done(((f32[16,256,128]{2,1,0:T(8,128)}), f32[16,256,128]{2,1,0:T(8,128)S(1)}, u32[]{:S(2)}, u32[]{:S(2)}) %all-to-all-start) | async-done | bytes 2097184 | tf_op jit(solution)/shard_map/all_to_all | solution.py:319
  46.7 2.1 %scan.1 = f32[16,264,128]{2,1,0:T(8,128)} custom-call(s32[1]{0:T(128)} %bitcast.spot_ref, f32[16,256,128]{2,1,0:T(8,128)S(1)} %all-to-all-done.own_ref, f32[8,128]{1,0:T(8,128)} %get-tuple-element.14.local_ref), custom_call_target="tpu_custom_call" | custom-call | flops 1572864 | bytes 4194304 | tf_op jit(solution)/shard_map/scan/pallas_call | solution.py:244
  48.9 0.0 copy-start
  48.9 31.6 %all_to_all.15.state_ref = f32[16,264,128]{2,1,0:T(8,128)S(1)} all-to-all(f32[16,264,128]{2,1,0:T(8,128)} %scan.1), channel_id=1, replica_groups=mesh['dp'=8,'ctx'=16] {'ctx'}, dimensions={0} | all-to-all | bytes 4325376 | tf_op jit(solution)/shard_map/all_to_all | solution.py:319
  80.4 0.6 gathered.1
  81.1 6.9 %all-to-all-start.2 = ((f32[8,8,128]{2,1,0:T(8,128)}), f32[8,8,128]{2,1,0:T(8,128)S(1)}, u32[]{:S(2)}, u32[]{:S(2)}) async-start(f32[8,8,128]{2,1,0:T(8,128)} %gathered.1), calls=%async_computation.2 | async-start | bytes 65536 | tf_op jit(solution)/shard_map/all_to_all | solution.py:319
  88.0 0.0 copy-done
  88.0 11.9 %far.1 = (bf16[1,768,2048]{2,1,0:T(8,128)(2,1)}, bf16[1,768,2048]{2,1,0:T(8,128)(2,1)}, bf16[1,768,2048]{2,1,0:T(8,128)(2,1)}) custom-call(f32[16]{0:T(128)S(1)} %copy-done, bf16[1,768,2048]{2,1,0:T(8,128)(2,1)} %k_ref.3, bf16[1,768,2048]{2,1,0:T(8,128)(2,1)} %v_ref.3, bf16[1,768,2048]{2,1,0:T(8,128)(2,1)} %g_ref.3, ...), custom_call_target="tpu_custom_call" | custom-call | flops 2415919104 | bytes 37748736 | tf_op jit(solution)/shard_map/far/pallas_call | solution.py:285
  99.9 0.0 all-to-all-done.2
  99.9 0.5 multiply_bitcast_fusion
  (1 shorter events, 0.0 us)
Async XLA Ops:
  7.3 39.4 %all-to-all-start = ((f32[16,256,128]{2,1,0:T(8,128)}), f32[16,256,128]{2,1,0:T(8,128)S(1)}, u32[]{:S(2)}, u32[]{:S(2)}) async-start(f32[16,256,128]{2,1,0:T(8,128)} %own_states.1), calls=%async_computation | async-start | bytes 4194304 | tf_op jit(solution)/shard_map/all_to_all | solution.py:319
  48.9 39.1 %copy-start = (f32[16]{0:T(128)S(1)}, f32[16]{0:T(128)}, u32[]{:S(2)}) copy-start(f32[16]{0:T(128)} %gain_ref.1) | copy-start | bytes 196
  81.1 18.8 %all-to-all-start.2 = ((f32[8,8,128]{2,1,0:T(8,128)}), f32[8,8,128]{2,1,0:T(8,128)S(1)}, u32[]{:S(2)}, u32[]{:S(2)}) async-start(f32[8,8,128]{2,1,0:T(8,128)} %gathered.1), calls=%async_computation.2 | async-start | bytes 65536 | tf_op jit(solution)/shard_map/all_to_all | solution.py:319
